TPU v7x, 128 devices: a whole 4x4x4 slice. The times are simulated.
128 devices in a mesh: dom: 128 (over z, y, x, core).
Axes of the slice: x: 4, y: 4, z: 4, core: 2. Of those that a mesh axis runs over, the one named last changes fastest.
Arguments:
- solution: float32 [4, 20, 262144], P(None, None, 'dom'), may hold values from -6 to 6
- register: float32 [4, 20, 262144], P(None, None, 'dom'), may hold values from -4 to 4
- geometry: float32 [9, 262144], P(None, 'dom'), may hold values from -4 to 4
- normals: float32 [3, 4, 262144], P(None, None, 'dom'), may hold values from -1 to 1, as said below
- face_scale: float32 [4, 262144], P(None, 'dom'), may hold values from 0.5 to 2
- impedance: float32 [16], replicated, may hold values from 0.2 to 5
- neighbour: int32 [4, 262144], P(None, 'dom'), may hold values from -1 to 9215
- orientation: int32 [4, 262144], P(None, 'dom'), may hold values from 0 to 2
- wall_material: int32 [4, 262144], P(None, 'dom'), may hold values from 0 to 15
- send_faces: int32 [1024, 128], P('dom'), may hold values from -1 to 8191, as said below
Outputs:
- solution_next: float32 [4, 20, 262144], P(None, None, 'dom')
- register_next: float32 [4, 20, 262144], P(None, None, 'dom')
- absorbed: float32 [2, 16], replicated
Inputs may be any that keep to these rules, and one draw needn't show every extreme that they name: `send_faces`: row j of partition d lists distinct local faces (numbered f * 2048 + e) sent to partition d + o_j in slot order, then -1; rows for partitions outside the mesh are all -1; the lists of two partitions for each other have equal lengths, and at most 128 faces go from one partition to another, a bound that is reached. Each face's three entries form a unit vector, and two faces that name each other as neighbours have opposite normals.
All inputs are finite; a program needn't handle non-finite values.
Results may differ from a plain program's by a relative error of at most 0.0003.
Values sent between devices are 32-bit elements; how exact they have to be, the bound alone decides.
No kernel may reach another device: no remote copies, remote signals or barrier semaphores. Data moves between devices by JAX's collectives and lax.ppermute only.
A program may use at most 128 MiB of HBM per device.

v0:
```python
import math

import jax
import jax.numpy as jnp
from jax import lax
from jax.sharding import PartitionSpec as P

NMAT = 16


section_decay = (-567301805773.0 / 1357537059087.0, -2404267990393.0 / 2016746695238.0)
section_weight = (1720146321549.0 / 2090206949498.0, 3134564353537.0 / 4481467310338.0)
time_step = 0.002


def passed_along(value, axis, by):
    devices = lax.axis_size(axis)
    pairs = [(i, i + by) for i in range(devices) if 0 <= i + by < devices]
    return lax.ppermute(value, axis, pairs)


def mat_product(left, right):
    inner = len(right)
    return [
        [sum((left[i][k] * right[k][j] for k in range(inner))) for j in range(len(right[0]))]
        for i in range(len(left))
    ]


def flipped(matrix):
    return [list(row) for row in zip(*matrix)]


def solve_rows(matrix, right):
    size = len(matrix)
    augmented = [list(matrix[i]) + list(right[i]) for i in range(size)]
    for column in range(size):
        pivot = max(range(column, size), key=lambda r: abs(augmented[r][column]))
        augmented[column], augmented[pivot] = (augmented[pivot], augmented[column])
        leader = augmented[column][column]
        augmented[column] = [value / leader for value in augmented[column]]
        for other in range(size):
            if other != column:
                factor = augmented[other][column]
                if factor != 0.0:
                    augmented[other] = [
                        a - factor * b for a, b in zip(augmented[other], augmented[column])
                    ]
    return [row[size:] for row in augmented]


def identity_rows(size):
    return [[1.0 if i == j else 0.0 for j in range(size)] for i in range(size)]


def dg_tables():
    lattice = [(i, j, k) for i in range(4) for j in range(4 - i) for k in range(4 - i - j)]
    coords = [(i / 3.0, j / 3.0, k / 3.0) for i, j, k in lattice]
    vander = [[x**a * y**b * z**c for a, b, c in lattice] for x, y, z in coords]
    inverse = solve_rows(vander, identity_rows(20))
    gradient_rows = []
    for d in range(3):
        derived = []
        for point in coords:
            row = []
            for powers in lattice:
                if powers[d] == 0:
                    row.append(0.0)
                else:
                    lowered = [powers[0], powers[1], powers[2]]
                    lowered[d] = lowered[d] - 1
                    row.append(
                        powers[d]
                        * point[0] ** lowered[0]
                        * point[1] ** lowered[1]
                        * point[2] ** lowered[2]
                    )
            derived.append(row)
        gradient_rows.extend(mat_product(derived, inverse))
    mono_mass = [
        [
            math.factorial(a + p)
            * math.factorial(b + q)
            * math.factorial(c + r)
            / math.factorial(a + b + c + p + q + r + 3)
            for p, q, r in lattice
        ]
        for a, b, c in lattice
    ]
    mass_matrix = mat_product(mat_product(flipped(inverse), mono_mass), inverse)
    plane_points = [(a, b) for a in range(4) for b in range(4 - a)]
    face_coords = [(a / 3.0, b / 3.0) for a, b in plane_points]
    vander_face = [[x**a * y**b for a, b in plane_points] for x, y in face_coords]
    inverse_face = solve_rows(vander_face, identity_rows(10))
    mono_face = [
        [
            math.factorial(a + p) * math.factorial(b + q) / math.factorial(a + b + p + q + 2)
            for p, q in plane_points
        ]
        for a, b in plane_points
    ]
    face_mass = mat_product(mat_product(flipped(inverse_face), mono_face), inverse_face)
    position = {point: n for n, point in enumerate(lattice)}
    builders = [
        lambda a, b: (a, b, 0),
        lambda a, b: (a, 0, b),
        lambda a, b: (0, a, b),
        lambda a, b: (a, b, 3 - a - b),
    ]
    face_nodes = [[position[builder(a, b)] for a, b in plane_points] for builder in builders]
    surface = [[0.0] * 40 for n in range(20)]
    for f in range(4):
        for n in range(10):
            for m in range(10):
                surface[face_nodes[f][n]][f * 10 + m] = face_mass[n][m]
    lift_matrix = solve_rows(mass_matrix, surface)
    rotations = []
    for t in range(3):
        mapping = []
        for a, b in plane_points:
            triple = (b, a, 3 - a - b)
            for s in range(t):
                triple = (triple[1], triple[2], triple[0])
            mapping.append(plane_points.index((triple[0], triple[1])))
        rotations.append(mapping)
    return (gradient_rows, lift_matrix, face_nodes, rotations)


def peer_offsets(half_span):
    return [j - half_span if j < half_span else j - half_span + 1 for j in range(2 * half_span)]


def node_major_traces(solution, node_order):
    elem_count = solution.shape[2]
    return solution[:, node_order, :].reshape(4, 10, 4 * elem_count)


def orient_values(values, orientation, rotate_tables):
    turned = jnp.einsum("tnk,fkx->tfnx", rotate_tables, values, precision=lax.Precision.HIGHEST)
    return jnp.where(orientation == 0, turned[0], jnp.where(orientation == 1, turned[1], turned[2]))


def wall_reflection(materials, impedance):
    material_ids = jnp.arange(impedance.shape[0], dtype=jnp.int32)
    picked = jnp.sum(
        jnp.where(
            materials[None, :] == material_ids[:, None], impedance[:, None], jnp.float32(0.0)
        ),
        axis=0,
    )
    return (picked - 1.0) / (picked + 1.0)


def face_flux(inner_trace, outer_trace, wall_mask, normal_flat, scale_flat, reflect):
    press_in = inner_trace[0]
    press_out = outer_trace[0]
    normal_in = (
        normal_flat[0] * inner_trace[1]
        + normal_flat[1] * inner_trace[2]
        + normal_flat[2] * inner_trace[3]
    )
    normal_out = (
        normal_flat[0] * outer_trace[1]
        + normal_flat[1] * outer_trace[2]
        + normal_flat[2] * outer_trace[3]
    )
    jump_press = jnp.where(wall_mask, (1.0 - reflect) * press_in, press_in - press_out)
    jump_normal = jnp.where(wall_mask, (1.0 + reflect) * normal_in, normal_in - normal_out)
    flux_press = 0.5 * scale_flat * (jump_normal - jump_press)
    flux_stack = jnp.stack(
        [
            flux_press,
            -normal_flat[0] * flux_press,
            -normal_flat[1] * flux_press,
            -normal_flat[2] * flux_press,
        ]
    )
    incoming = press_in + normal_in
    wall_loss = 0.25 * scale_flat * (1.0 - reflect * reflect) * incoming * incoming
    return (flux_stack, wall_loss)


def material_sums(wall_loss, wall_mask, materials, material_count):
    per_face = jnp.where(wall_mask, jnp.sum(wall_loss, axis=0), jnp.float32(0.0))
    material_ids = jnp.arange(material_count, dtype=jnp.int32)
    return jnp.sum(
        jnp.where(materials[None, :] == material_ids[:, None], per_face[None, :], jnp.float32(0.0)),
        axis=1,
    )


def assemble(solution, geometry, flux_stack, gradient_ops, lift_node_major):
    elem_count = solution.shape[2]
    gradients = jnp.einsum(
        "km,fme->fke", gradient_ops, solution, precision=lax.Precision.HIGHEST
    ).reshape(4, 3, 20, elem_count)
    metric = geometry.reshape(3, 3, elem_count)

    def physical_derivative(field_index, i):
        return (
            metric[i, 0] * gradients[field_index, 0]
            + metric[i, 1] * gradients[field_index, 1]
            + metric[i, 2] * gradients[field_index, 2]
        )

    flux_faces = flux_stack.reshape(4, 40, elem_count)
    lifted = jnp.einsum("nk,fke->fne", lift_node_major, flux_faces, precision=lax.Precision.HIGHEST)
    divergence = physical_derivative(1, 0) + physical_derivative(2, 1) + physical_derivative(3, 2)
    return jnp.stack(
        [
            lifted[0] - divergence,
            lifted[1] - physical_derivative(0, 0),
            lifted[2] - physical_derivative(0, 1),
            lifted[3] - physical_derivative(0, 2),
        ]
    )


def local(
    solution,
    register,
    geometry,
    normals,
    face_scale,
    impedance,
    neighbour,
    orientation,
    wall_material,
    send_faces,
):
    grad_rows, lift_rows, face_nodes, rotations = dg_tables()
    gradient_ops = jnp.asarray(grad_rows, dtype=jnp.float32)
    lift_reordered = [[row[f * 10 + m] for m in range(10) for f in range(4)] for row in lift_rows]
    lift_node_major = jnp.asarray(lift_reordered, dtype=jnp.float32)
    node_order = jnp.array([face_nodes[f][m] for m in range(10) for f in range(4)], dtype=jnp.int32)
    rotate_tables = jnp.asarray(
        [
            [[1.0 if rotations[t][n] == k else 0.0 for k in range(10)] for n in range(10)]
            for t in range(3)
        ],
        dtype=jnp.float32,
    )
    elem_count = solution.shape[2]
    face_count = 4 * elem_count
    blocks = send_faces.shape[0]
    capacity = send_faces.shape[1]
    offsets = peer_offsets(blocks // 2)
    devices = lax.axis_size("dom")
    link_codes = neighbour.reshape(face_count)
    orient_flat = orientation.reshape(face_count)
    materials = wall_material.reshape(face_count)
    wall_mask = link_codes < 0
    reflect = wall_reflection(materials, impedance)
    normal_flat = normals.reshape(3, face_count)
    scale_flat = face_scale.reshape(face_count)
    gather_index = jnp.maximum(link_codes, 0)
    send_index = jnp.maximum(send_faces, 0)
    send_live = send_faces >= 0
    norm_factor = NMAT / (devices * elem_count)
    absorbed = []
    for section_index in range(2):
        inner_trace = node_major_traces(solution, node_order)
        flat_inner = inner_trace.reshape(40, face_count)
        outgoing = jnp.where(
            send_live[None], jnp.take(flat_inner, send_index, axis=1), jnp.float32(0.0)
        )
        pieces = []
        for j in range(blocks):
            pieces.append(passed_along(outgoing[:, blocks - 1 - j], "dom", -offsets[j]))
        incoming = jnp.stack(pieces, axis=1)
        trace_table = jnp.concatenate([flat_inner, incoming.reshape(40, blocks * capacity)], axis=1)
        outer_trace = jnp.take(trace_table, gather_index, axis=1).reshape(4, 10, face_count)
        outer_trace = orient_values(outer_trace, orient_flat, rotate_tables)
        flux_stack, wall_loss = face_flux(
            inner_trace, outer_trace, wall_mask, normal_flat, scale_flat, reflect
        )
        rhs_local = assemble(solution, geometry, flux_stack, gradient_ops, lift_node_major)
        totals = material_sums(wall_loss, wall_mask, materials, impedance.shape[0])
        absorbed.append(lax.psum(totals, "dom") * norm_factor)
        register = section_decay[section_index] * register + time_step * rhs_local
        solution = solution + section_weight[section_index] * register
    absorbed_out = jnp.stack(absorbed)
    return (solution, register, absorbed_out)


def solution(mesh):
    in_specs = (
        P(None, None, "dom"),
        P(None, None, "dom"),
        P(None, "dom"),
        P(None, None, "dom"),
        P(None, "dom"),
        P(),
        P(None, "dom"),
        P(None, "dom"),
        P(None, "dom"),
        P("dom", None),
    )
    out_specs = (P(None, None, "dom"), P(None, None, "dom"), P())
    return jax.shard_map(local, mesh=mesh, in_specs=in_specs, out_specs=out_specs, check_vma=False)
```

profile of v0, /device:TPU:33, one launch (start us, length us, event | category | flops | bytes accessed | tf_op | source)
XLA Modules:
  0.0 331.8 jit_solution(7664789886038245700)
XLA Ops:
  2.7 2.4 gather_fusion
  5.1 1.8 copy.173
  7.0 1.9 reshape_reshape.6
  8.8 2.7 copy.174
  11.6 5.0 %gather_fusion.2 = f32[1024,40]{1,0:T(8,128)S(1)} fusion(f32[40,8192]{0,1:T(8,128)} %copy.174, s32[1024]{0:T(1024)S(1)} %bitcast_clamp_fusion), kind=kCustom, calls=%fused_computation.clone | custom fusion | bytes 331776 | tf_op jit(solution)/shard_map/jit(_take)/gather | solution.py:265
  17.6 3.1 collective-permute-start.2
  20.7 4.0 %collective-permute-start.3 = (f32[40,128]{1,0:T(8,128)}, f32[40,128]{1,0:T(8,128)}, u32[]{:S(2)}, u32[]{:S(2)}) collective-permute-start(f32[40,128]{1,0:T(8,128)} %get-tuple-element.86), channel_id=1, source_target_pairs={{0,1},{1,2},{2,3},{3,4},{4,5},{5,6},{6,7},{7,8},{8,9},{9,10},{10,1... | collective-permute-start | bytes 61448 | tf_op jit(solution)/shard_map/ppermute | solution.py:19
  24.6 1.9 collective-permute-start.4
  26.6 6.4 %collective-permute-start.5 = (f32[40,128]{1,0:T(8,128)}, f32[40,128]{1,0:T(8,128)}, u32[]{:S(2)}, u32[]{:S(2)}) collective-permute-start(f32[40,128]{1,0:T(8,128)} %get-tuple-element.84), channel_id=1, source_target_pairs={{2,0},{3,1},{4,2},{5,3},{6,4},{7,5},{8,6},{9,7},{10,8},{11,9},{12,... | collective-permute-start | bytes 61448 | tf_op jit(solution)/shard_map/ppermute | solution.py:19
  33.0 3.1 collective-permute-start.6
  36.1 4.3 %slice_reduce_fusion.7 = (f32[40,2048]{1,0:T(8,128)}, f32[40,2048]{1,0:T(8,128)}, f32[40,2048]{1,0:T(8,128)}, f32[40,2048]{1,0:T(8,128)}) fusion(f32[4,40,2048]{2,0,1:T(4,128)S(1)} %bitcast.454), kind=kLoop, calls=%fused_computation.86 | loop fusion | bytes 2621440 | tf_op jit(solution)/shard_map/slice | solution.py:158
  41.8 2.0 convolution_bitcast_fusion.3
  43.8 1.3 copy.188
  45.1 2.7 fusion.109
  50.0 4.5 %collective-permute-start.7 = (f32[40,128]{1,0:T(8,128)}, f32[40,128]{1,0:T(8,128)}, u32[]{:S(2)}, u32[]{:S(2)}) collective-permute-start(f32[40,128]{1,0:T(8,128)} %get-tuple-element.82), channel_id=1, source_target_pairs={{4,0},{5,1},{6,2},{7,3},{8,4},{9,5},{10,6},{11,7},{12,8},{13,9},{1... | collective-permute-start | bytes 61448 | tf_op jit(solution)/shard_map/ppermute | solution.py:19
  54.5 2.2 collective-permute-start
  56.8 6.0 %collective-permute-start.1 = (f32[40,128]{1,0:T(8,128)}, f32[40,128]{1,0:T(8,128)}, u32[]{:S(2)}, u32[]{:S(2)}) collective-permute-start(f32[40,128]{1,0:T(8,128)} %get-tuple-element.88), channel_id=1, source_target_pairs={{0,3},{1,4},{2,5},{3,6},{4,7},{5,8},{6,9},{7,10},{8,11},{9,12},{10... | collective-permute-start | bytes 61448 | tf_op jit(solution)/shard_map/ppermute | solution.py:19
  64.3 0.9 squeeze.266
  65.3 1.0 squeeze.212
  66.3 0.9 squeeze.267
  69.1 0.9 squeeze.214
  70.0 1.0 squeeze.269
  74.1 1.1 stack.115
  75.2 1.2 pad_maximum_fusion
  76.4 4.0 %copy.183 = f32[40,9216]{0,1:T(8,128)} copy(f32[40,9216]{1,0:T(8,128)} %pad_maximum_fusion) | data formatting | bytes 2949120 | tf_op jit(solution)/shard_map/concatenate | solution.py:271
  80.4 30.0 %gather_fusion.3 = f32[8192,40]{1,0:T(8,128)} fusion(f32[40,9216]{0,1:T(8,128)} %copy.183, s32[8192]{0:T(1024)S(1)} %fusion.102), kind=kCustom, calls=%fused_computation.1.clone | custom fusion | bytes 2654208 | tf_op jit(solution)/shard_map/jit(_take)/gather | solution.py:272
  110.4 7.5 %select_bitcast_fusion.1 = f32[40,8192]{0,1:T(8,128)} fusion(f32[8192,40]{1,0:T(8,128)} %gather_fusion.3, pred[8192]{0:T(1024)(128)(4,1)S(1)} %copy-done.99), kind=kLoop, calls=%fused_computation.9 | loop fusion | flops 327680 | bytes 2629632 | tf_op jit(solution)/shard_map/jit(_take)/select_n | solution.py:272
  117.9 3.7 %copy.184 = f32[40,8192]{1,0:T(8,128)} copy(f32[40,8192]{0,1:T(8,128)} %select_bitcast_fusion.1) | data formatting | bytes 2621440 | tf_op jit(solution)/shard_map/jit(_take)/select_n | solution.py:272
  121.6 1.5 reshape.2565
  123.1 5.8 %convolution_bitcast_fusion.1 = f32[3,4,10,8192]{3,2,0,1:T(8,128)S(1)} fusion(f32[3,10,10,1]{2,1,0,3:T(8,128)S(1)} %copy-done.113, f32[4,10,8192,1]{2,1,0,3:T(8,128)S(1)} %reshape.2565), kind=kOutput, calls=%fused_computation.7 | convolution fusion | flops 117964800 | bytes 5244080 | tf_op jit(solution)/shard_map/tnk,fkx->tfnx/dot_general | solution.py:139
  130.5 1.1 broadcast_multiply_fusion.5
  134.6 2.1 convolution_bitcast_fusion.5
  139.2 1.5 gather_fusion.1
  140.6 4.5 %slice_reduce_fusion.3 = (f32[40,2048]{1,0:T(8,128)}, f32[40,2048]{1,0:T(8,128)}, f32[40,2048]{1,0:T(8,128)}, f32[40,2048]{1,0:T(8,128)}) fusion(f32[4,40,2048]{2,0,1:T(4,128)S(1)} %bitcast.455), kind=kLoop, calls=%fused_computation.82 | loop fusion | bytes 2621440 | tf_op jit(solution)/shard_map/slice | solution.py:158
  145.9 3.3 convolution_bitcast_fusion.2
  149.2 0.9 squeeze.270
  150.1 1.0 squeeze.271
  151.1 1.0 squeeze.272
  153.7 2.7 copy.204
  156.4 5.0 %gather_fusion.4 = f32[1024,40]{1,0:T(8,128)S(1)} fusion(f32[40,8192]{0,1:T(8,128)} %copy.204, s32[1024]{0:T(1024)S(1)} %copy-done.108), kind=kCustom, calls=%fused_computation.2.clone | custom fusion | bytes 331776 | tf_op jit(solution)/shard_map/jit(_take)/gather | solution.py:265
  162.3 1.9 collective-permute-start.8
  164.3 1.9 collective-permute-start.9
  166.2 4.0 %collective-permute-start.10 = (f32[40,128]{1,0:T(8,128)}, f32[40,128]{1,0:T(8,128)}, u32[]{:S(2)}, u32[]{:S(2)}) collective-permute-start(f32[40,128]{1,0:T(8,128)} %get-tuple-element.79), channel_id=1, source_target_pairs={{0,2},{1,3},{2,4},{3,5},{4,6},{5,7},{6,8},{7,9},{8,10},{9,11},{10,... | collective-permute-start | bytes 61448 | tf_op jit(solution)/shard_map/ppermute | solution.py:19
  170.2 1.9 collective-permute-start.11
  172.1 2.4 collective-permute-start.12
  174.5 2.9 copy.217
  177.5 2.7 fusion.108
  181.9 68.8 %all-reduce = (f32[16]{0:T(128)}, f32[16]{0:T(128)}) all-reduce(f32[16]{0:T(128)} %get-tuple-element.31, f32[16]{0:T(128)} %get-tuple-element.30), channel_id=1, replica_groups=mesh['dom'=128] {'dom'}, use_global_device_ids=true, to_apply=%region_6.9 | all-reduce | flops 32 | bytes 256 | tf_op jit(solution)/shard_map/psum | solution.py:279
  251.4 4.2 %collective-permute-start.13 = (f32[40,128]{1,0:T(8,128)}, f32[40,128]{1,0:T(8,128)}, u32[]{:S(2)}, u32[]{:S(2)}) collective-permute-start(f32[40,128]{1,0:T(8,128)} %get-tuple-element.76), channel_id=1, source_target_pairs={{2,0},{3,1},{4,2},{5,3},{6,4},{7,5},{8,6},{9,7},{10,8},{11,9},{12,... | collective-permute-start | bytes 61448 | tf_op jit(solution)/shard_map/ppermute | solution.py:19
  255.6 3.6 %collective-permute-start.14 = (f32[40,128]{1,0:T(8,128)}, f32[40,128]{1,0:T(8,128)}, u32[]{:S(2)}, u32[]{:S(2)}) collective-permute-start(f32[40,128]{1,0:T(8,128)} %get-tuple-element.75), channel_id=1, source_target_pairs={{3,0},{4,1},{5,2},{6,3},{7,4},{8,5},{9,6},{10,7},{11,8},{12,9},{13... | collective-permute-start | bytes 61448 | tf_op jit(solution)/shard_map/ppermute | solution.py:19
  259.2 4.0 %collective-permute-start.15 = (f32[40,128]{1,0:T(8,128)}, f32[40,128]{1,0:T(8,128)}, u32[]{:S(2)}, u32[]{:S(2)}) collective-permute-start(f32[40,128]{1,0:T(8,128)} %get-tuple-element.74), channel_id=1, source_target_pairs={{4,0},{5,1},{6,2},{7,3},{8,4},{9,5},{10,6},{11,7},{12,8},{13,9},{1... | collective-permute-start | bytes 61448 | tf_op jit(solution)/shard_map/ppermute | solution.py:19
  263.8 0.9 squeeze.239
  265.9 0.9 squeeze.253
  266.8 1.1 stack.130
  268.0 1.2 pad_maximum_fusion.1
  269.2 4.0 %copy.214 = f32[40,9216]{0,1:T(8,128)} copy(f32[40,9216]{1,0:T(8,128)} %pad_maximum_fusion.1) | data formatting | bytes 2949120 | tf_op jit(solution)/shard_map/concatenate | solution.py:271
  273.2 30.0 %gather_fusion.5 = f32[8192,40]{1,0:T(8,128)} fusion(f32[40,9216]{0,1:T(8,128)} %copy.214, s32[8192]{0:T(1024)S(1)} %copy-done.66), kind=kCustom, calls=%fused_computation.3.clone | custom fusion | bytes 2654208 | tf_op jit(solution)/shard_map/jit(_take)/gather | solution.py:272
  303.2 7.5 %select_bitcast_fusion = f32[40,8192]{0,1:T(8,128)} fusion(f32[8192,40]{1,0:T(8,128)} %gather_fusion.5, pred[8192]{0:T(1024)(128)(4,1)S(1)} %copy-done.100), kind=kLoop, calls=%fused_computation.8 | loop fusion | flops 327680 | bytes 2629632 | tf_op jit(solution)/shard_map/jit(_take)/select_n | solution.py:272
  310.7 3.7 %copy.215 = f32[40,8192]{1,0:T(8,128)} copy(f32[40,8192]{0,1:T(8,128)} %select_bitcast_fusion) | data formatting | bytes 2621440 | tf_op jit(solution)/shard_map/jit(_take)/select_n | solution.py:272
  314.3 1.5 reshape.2569
  315.9 6.6 %convolution_bitcast_fusion = f32[3,4,10,8192]{3,2,1,0:T(8,128)S(1)} fusion(f32[4,10,8192,1]{2,1,0,3:T(8,128)S(1)} %reshape.2569, f32[3,10,10,1]{2,1,3,0:T(8,128)} %constant.76), kind=kOutput, calls=%fused_computation.6 | convolution fusion | flops 117964800 | bytes 5244080 | tf_op jit(solution)/shard_map/tnk,fkx->tfnx/dot_general | solution.py:139
  325.3 1.7 convolution_bitcast_fusion.4
  329.0 1.3 copy.230
  330.3 1.3 copy.231
  (326 shorter events, 31.0 us)
Async XLA Ops:
  1.3 10.3 %copy-start.107 = (s32[1024]{0:T(1024)}, s32[1024]{0:T(1024)S(1)}, u32[]{:S(2)}) copy-start(s32[1024]{0:T(1024)S(1)} %bitcast_clamp_fusion) | copy-start | bytes 12292
  2.0 14.8 %copy-start.114 = (pred[8,128]{1,0:T(8,128)(4,1)}, pred[8,128]{1,0:T(8,128)(4,1)S(1)}, u32[]{:S(2)}) copy-start(pred[8,128]{1,0:T(8,128)(4,1)S(1)} %get-tuple-element.111) | copy-start | bytes 3076
  2.0 14.8 %copy-start.116 = (pred[8,128]{1,0:T(8,128)(4,1)}, pred[8,128]{1,0:T(8,128)(4,1)S(1)}, u32[]{:S(2)}) copy-start(pred[8,128]{1,0:T(8,128)(4,1)S(1)} %get-tuple-element.112) | copy-start | bytes 3076
  2.7 4.3 %copy-start.118 = (s32[1024]{0:T(1024)}, s32[1024]{0:T(1024)S(1)}, u32[]{:S(2)}) copy-start(s32[1024]{0:T(1024)S(1)} %pad_clamp_fusion) | copy-start | bytes 12292
  16.6 23.8 %copy-start.96 = (s32[4,2048]{1,0:T(4,128)S(1)}, s32[4,2048]{1,0:T(4,128)}, u32[]{:S(2)}) copy-start(s32[4,2048]{1,0:T(4,128)} %param.24) | copy-start | bytes 98308
  16.6 23.9 %copy-start.111 = (s32[4,2048]{1,0:T(4,128)S(1)}, s32[4,2048]{1,0:T(4,128)}, u32[]{:S(2)}) copy-start(s32[4,2048]{1,0:T(4,128)} %param.25) | copy-start | bytes 98308
  16.6 24.5 %copy-start.109 = (f32[4,2048]{1,0:T(4,128)S(1)}, f32[4,2048]{1,0:T(4,128)}, u32[]{:S(2)}) copy-start(f32[4,2048]{1,0:T(4,128)} %param.22) | copy-start | bytes 98308
  16.8 23.7 %copy-start.98 = (f32[3,4,2048]{2,1,0:T(4,128)S(1)}, f32[3,4,2048]{2,1,0:T(4,128)}, u32[]{:S(2)}) copy-start(f32[3,4,2048]{2,1,0:T(4,128)} %param.21) | copy-start | bytes 294916
  16.8 25.0 %copy-start.112 = (s32[4,2048]{1,0:T(4,128)S(1)}, s32[4,2048]{1,0:T(4,128)}, u32[]{:S(2)}) copy-start(s32[4,2048]{1,0:T(4,128)} %param.26) | copy-start | bytes 98308
  16.8 24.9 %copy-start = (f32[4,20,2048]{2,0,1:T(4,128)S(1)}, f32[4,20,2048]{2,0,1:T(4,128)}, u32[]{:S(2)}) copy-start(f32[4,20,2048]{2,0,1:T(4,128)} %param.18) | copy-start | bytes 1966084
  16.8 24.9 %copy-start.105 = (f32[60,20,1]{0,1,2:T(8,128)S(1)}, f32[60,20,1]{0,1,2:T(8,128)}, u32[]{:S(2)}) copy-start(f32[60,20,1]{0,1,2:T(8,128)} %constant.75) | copy-start | bytes 14404
  17.6 32.4 %collective-permute-start.2 = (f32[40,128]{1,0:T(8,128)}, f32[40,128]{1,0:T(8,128)}, u32[]{:S(2)}, u32[]{:S(2)}) collective-permute-start(f32[40,128]{1,0:T(8,128)} %get-tuple-element.87), channel_id=1, source_target_pairs={{0,2},{1,3},{2,4},{3,5},{4,6},{5,7},{6,8},{7,9},{8,10},{9,11},{10,... | collective-permute-start | bytes 61448 | tf_op jit(solution)/shard_map/ppermute | solution.py:19
  20.7 33.8 %collective-permute-start.3 = (f32[40,128]{1,0:T(8,128)}, f32[40,128]{1,0:T(8,128)}, u32[]{:S(2)}, u32[]{:S(2)}) collective-permute-start(f32[40,128]{1,0:T(8,128)} %get-tuple-element.86), channel_id=1, source_target_pairs={{0,1},{1,2},{2,3},{3,4},{4,5},{5,6},{6,7},{7,8},{8,9},{9,10},{10,1... | collective-permute-start | bytes 61448 | tf_op jit(solution)/shard_map/ppermute | solution.py:19
  24.6 32.1 %collective-permute-start.4 = (f32[40,128]{1,0:T(8,128)}, f32[40,128]{1,0:T(8,128)}, u32[]{:S(2)}, u32[]{:S(2)}) collective-permute-start(f32[40,128]{1,0:T(8,128)} %get-tuple-element.85), channel_id=1, source_target_pairs={{1,0},{2,1},{3,2},{4,3},{5,4},{6,5},{7,6},{8,7},{9,8},{10,9},{11,1... | collective-permute-start | bytes 61448 | tf_op jit(solution)/shard_map/ppermute | solution.py:19
  26.6 47.5 %collective-permute-start.5 = (f32[40,128]{1,0:T(8,128)}, f32[40,128]{1,0:T(8,128)}, u32[]{:S(2)}, u32[]{:S(2)}) collective-permute-start(f32[40,128]{1,0:T(8,128)} %get-tuple-element.84), channel_id=1, source_target_pairs={{2,0},{3,1},{4,2},{5,3},{6,4},{7,5},{8,6},{9,7},{10,8},{11,9},{12,... | collective-permute-start | bytes 61448 | tf_op jit(solution)/shard_map/ppermute | solution.py:19
  33.0 41.1 %collective-permute-start.6 = (f32[40,128]{1,0:T(8,128)}, f32[40,128]{1,0:T(8,128)}, u32[]{:S(2)}, u32[]{:S(2)}) collective-permute-start(f32[40,128]{1,0:T(8,128)} %get-tuple-element.83), channel_id=1, source_target_pairs={{3,0},{4,1},{5,2},{6,3},{7,4},{8,5},{9,6},{10,7},{11,8},{12,9},{13... | collective-permute-start | bytes 61448 | tf_op jit(solution)/shard_map/ppermute | solution.py:19
  40.5 39.9 %copy-start.65 = (s32[8192]{0:T(1024)}, s32[8192]{0:T(1024)S(1)}, u32[]{:S(2)}) copy-start(s32[8192]{0:T(1024)S(1)} %fusion.102) | copy-start | bytes 98308
  41.8 6.8 %copy-start.74 = (s32[1,16,4,128]{3,1,2,0:T(8,128)}, s32[1,16,4,128]{3,1,2,0:T(8,128)S(1)}, u32[]{:S(2)}) copy-start(s32[1,16,4,128]{3,1,2,0:T(8,128)S(1)} %copy.263) | copy-start | bytes 98308
  45.1 3.4 %copy-start.119 = (f32[16]{0:T(128)S(1)}, f32[16]{0:T(128)}, u32[]{:S(2)}) copy-start(f32[16]{0:T(128)} %param.23) | copy-start | bytes 196
  45.1 18.2 %copy-start.12 = (f32[40,2048]{1,0:T(8,128)S(1)}, f32[40,2048]{1,0:T(8,128)}, u32[]{:S(2)}) copy-start(f32[40,2048]{1,0:T(8,128)} %get-tuple-element.27) | copy-start | bytes 983044
  47.8 17.4 %copy-start.11 = (f32[40,2048]{1,0:T(8,128)S(1)}, f32[40,2048]{1,0:T(8,128)}, u32[]{:S(2)}) copy-start(f32[40,2048]{1,0:T(8,128)} %get-tuple-element.24) | copy-start | bytes 983044
  47.8 19.4 %copy-start.10 = (f32[40,2048]{1,0:T(8,128)S(1)}, f32[40,2048]{1,0:T(8,128)}, u32[]{:S(2)}) copy-start(f32[40,2048]{1,0:T(8,128)} %get-tuple-element.26) | copy-start | bytes 983044
  49.4 80.0 %copy-start.63 = (f32[8192]{0:T(1024)}, f32[8192]{0:T(1024)S(1)}, u32[]{:S(2)}) copy-start(f32[8192]{0:T(1024)S(1)} %get-tuple-element.104) | copy-start | bytes 98308
  50.0 24.1 %collective-permute-start.7 = (f32[40,128]{1,0:T(8,128)}, f32[40,128]{1,0:T(8,128)}, u32[]{:S(2)}, u32[]{:S(2)}) collective-permute-start(f32[40,128]{1,0:T(8,128)} %get-tuple-element.82), channel_id=1, source_target_pairs={{4,0},{5,1},{6,2},{7,3},{8,4},{9,5},{10,6},{11,7},{12,8},{13,9},{1... | collective-permute-start | bytes 61448 | tf_op jit(solution)/shard_map/ppermute | solution.py:19
  54.5 19.6 %collective-permute-start = (f32[40,128]{1,0:T(8,128)}, f32[40,128]{1,0:T(8,128)}, u32[]{:S(2)}, u32[]{:S(2)}) collective-permute-start(f32[40,128]{1,0:T(8,128)} %get-tuple-element.89), channel_id=1, source_target_pairs={{0,4},{1,5},{2,6},{3,7},{4,8},{5,9},{6,10},{7,11},{8,12},{9,13},{1... | collective-permute-start | bytes 61448 | tf_op jit(solution)/shard_map/ppermute | solution.py:19
  56.8 17.3 %collective-permute-start.1 = (f32[40,128]{1,0:T(8,128)}, f32[40,128]{1,0:T(8,128)}, u32[]{:S(2)}, u32[]{:S(2)}) collective-permute-start(f32[40,128]{1,0:T(8,128)} %get-tuple-element.88), channel_id=1, source_target_pairs={{0,3},{1,4},{2,5},{3,6},{4,7},{5,8},{6,9},{7,10},{8,11},{9,12},{10... | collective-permute-start | bytes 61448 | tf_op jit(solution)/shard_map/ppermute | solution.py:19
  64.3 4.8 %copy-start.9 = (f32[40,2048]{1,0:T(8,128)S(1)}, f32[40,2048]{1,0:T(8,128)}, u32[]{:S(2)}) copy-start(f32[40,2048]{1,0:T(8,128)} %get-tuple-element.25) | copy-start | bytes 983044
  66.3 5.9 %copy-start.97 = (f32[1,16,4,128]{3,2,1,0:T(4,128)S(1)}, f32[1,16,4,128]{3,2,1,0:T(4,128)}, u32[]{:S(2)}) copy-start(f32[1,16,4,128]{3,2,1,0:T(4,128)} %get-tuple-element.100) | copy-start | bytes 98308
  66.3 6.0 %copy-start.95 = (f32[1,16,4,128]{3,2,1,0:T(4,128)S(1)}, f32[1,16,4,128]{3,2,1,0:T(4,128)}, u32[]{:S(2)}) copy-start(f32[1,16,4,128]{3,2,1,0:T(4,128)} %get-tuple-element.106) | copy-start | bytes 98308
  67.2 5.0 %copy-start.110 = (pred[1,16,4,128]{3,2,1,0:T(4,128)(4,1)S(1)}, pred[1,16,4,128]{3,2,1,0:T(4,128)(4,1)}, u32[]{:S(2)}) copy-start(pred[1,16,4,128]{3,2,1,0:T(4,128)(4,1)} %compare_bitcast_fusion.2) | copy-start | bytes 24580
  72.2 57.2 %copy-start.67 = (f32[8192]{0:T(1024)}, f32[8192]{0:T(1024)S(1)}, u32[]{:S(2)}) copy-start(f32[8192]{0:T(1024)S(1)} %neg.24) | copy-start | bytes 98308
  72.2 57.1 %copy-start.69 = (f32[1,16,4,128]{3,1,2,0:T(8,128)}, f32[1,16,4,128]{3,1,2,0:T(8,128)S(1)}, u32[]{:S(2)}) copy-start(f32[1,16,4,128]{3,1,2,0:T(8,128)S(1)} %copy.261) | copy-start | bytes 98308
  80.4 30.0 %copy-start.99 = (pred[8192]{0:T(1024)(128)(4,1)S(1)}, pred[8192]{0:T(1024)(128)(4,1)}, u32[]{:S(2)}) copy-start(pred[8192]{0:T(1024)(128)(4,1)} %compare_and_fusion) | copy-start | bytes 24580
  123.1 5.9 %copy-start.101 = (pred[1,16,4,128]{3,1,2,0:T(8,128)(4,1)S(1)}, pred[1,16,4,128]{3,1,2,0:T(8,128)(4,1)}, u32[]{:S(2)}) copy-start(pred[1,16,4,128]{3,1,2,0:T(8,128)(4,1)} %copy.267) | copy-start | bytes 24580
  123.1 5.9 %copy-start.103 = (pred[1,16,4,128]{3,1,2,0:T(8,128)(4,1)S(1)}, pred[1,16,4,128]{3,1,2,0:T(8,128)(4,1)}, u32[]{:S(2)}) copy-start(pred[1,16,4,128]{3,1,2,0:T(8,128)(4,1)} %copy.270) | copy-start | bytes 24580
  140.6 5.3 %copy-start.106 = (f32[60,20,1]{0,1,2:T(8,128)S(1)}, f32[60,20,1]{0,1,2:T(8,128)}, u32[]{:S(2)}) copy-start(f32[60,20,1]{0,1,2:T(8,128)} %constant.75) | copy-start | bytes 14404
  145.9 3.3 copy-start.1
  145.9 4.2 %copy-start.7 = (f32[40,2048]{1,0:T(8,128)S(1)}, f32[40,2048]{1,0:T(8,128)}, u32[]{:S(2)}) copy-start(f32[40,2048]{1,0:T(8,128)} %get-tuple-element.20) | copy-start | bytes 983044
  145.9 5.2 %copy-start.5 = (f32[40,2048]{1,0:T(8,128)S(1)}, f32[40,2048]{1,0:T(8,128)}, u32[]{:S(2)}) copy-start(f32[40,2048]{1,0:T(8,128)} %get-tuple-element.22) | copy-start | bytes 983044
  145.9 6.2 %copy-start.3 = (f32[40,2048]{1,0:T(8,128)S(1)}, f32[40,2048]{1,0:T(8,128)}, u32[]{:S(2)}) copy-start(f32[40,2048]{1,0:T(8,128)} %get-tuple-element.21) | copy-start | bytes 983044
  156.4 5.2 %copy-start.115 = (pred[8,128]{1,0:T(8,128)(4,1)S(1)}, pred[8,128]{1,0:T(8,128)(4,1)}, u32[]{:S(2)}) copy-start(pred[8,128]{1,0:T(8,128)(4,1)} %copy-done.114) | copy-start | bytes 3076
  156.4 5.2 %copy-start.117 = (pred[8,128]{1,0:T(8,128)(4,1)S(1)}, pred[8,128]{1,0:T(8,128)(4,1)}, u32[]{:S(2)}) copy-start(pred[8,128]{1,0:T(8,128)(4,1)} %copy-done.116) | copy-start | bytes 3076
  162.3 89.1 %collective-permute-start.8 = (f32[40,128]{1,0:T(8,128)}, f32[40,128]{1,0:T(8,128)}, u32[]{:S(2)}, u32[]{:S(2)}) collective-permute-start(f32[40,128]{1,0:T(8,128)} %get-tuple-element.81), channel_id=1, source_target_pairs={{0,4},{1,5},{2,6},{3,7},{4,8},{5,9},{6,10},{7,11},{8,12},{9,13},{1... | collective-permute-start | bytes 61448 | tf_op jit(solution)/shard_map/ppermute | solution.py:19
  164.3 91.4 %collective-permute-start.9 = (f32[40,128]{1,0:T(8,128)}, f32[40,128]{1,0:T(8,128)}, u32[]{:S(2)}, u32[]{:S(2)}) collective-permute-start(f32[40,128]{1,0:T(8,128)} %get-tuple-element.80), channel_id=1, source_target_pairs={{0,3},{1,4},{2,5},{3,6},{4,7},{5,8},{6,9},{7,10},{8,11},{9,12},{10... | collective-permute-start | bytes 61448 | tf_op jit(solution)/shard_map/ppermute | solution.py:19
  166.2 93.0 %collective-permute-start.10 = (f32[40,128]{1,0:T(8,128)}, f32[40,128]{1,0:T(8,128)}, u32[]{:S(2)}, u32[]{:S(2)}) collective-permute-start(f32[40,128]{1,0:T(8,128)} %get-tuple-element.79), channel_id=1, source_target_pairs={{0,2},{1,3},{2,4},{3,5},{4,6},{5,7},{6,8},{7,9},{8,10},{9,11},{10,... | collective-permute-start | bytes 61448 | tf_op jit(solution)/shard_map/ppermute | solution.py:19
  170.2 96.6 %collective-permute-start.11 = (f32[40,128]{1,0:T(8,128)}, f32[40,128]{1,0:T(8,128)}, u32[]{:S(2)}, u32[]{:S(2)}) collective-permute-start(f32[40,128]{1,0:T(8,128)} %get-tuple-element.78), channel_id=1, source_target_pairs={{0,1},{1,2},{2,3},{3,4},{4,5},{5,6},{6,7},{7,8},{8,9},{9,10},{10,1... | collective-permute-start | bytes 61448 | tf_op jit(solution)/shard_map/ppermute | solution.py:19
  172.1 94.7 %collective-permute-start.12 = (f32[40,128]{1,0:T(8,128)}, f32[40,128]{1,0:T(8,128)}, u32[]{:S(2)}, u32[]{:S(2)}) collective-permute-start(f32[40,128]{1,0:T(8,128)} %get-tuple-element.77), channel_id=1, source_target_pairs={{1,0},{2,1},{3,2},{4,3},{5,4},{6,5},{7,6},{8,7},{9,8},{10,9},{11,1... | collective-permute-start | bytes 61448 | tf_op jit(solution)/shard_map/ppermute | solution.py:19
  174.5 5.7 %copy-start.22 = (f32[10,8192]{1,0:T(8,128)S(1)}, f32[10,8192]{1,0:T(8,128)}, u32[]{:S(2)}) copy-start(f32[10,8192]{1,0:T(8,128)} %squeeze.273) | copy-start | bytes 983044
  177.5 2.8 copy-start.15
  177.5 2.8 copy-start.16
  177.5 2.8 copy-start.17
  177.5 2.8 copy-start.18
  177.5 2.8 copy-start.19
  180.4 83.5 %copy-start.8 = (f32[40,2048]{1,0:T(8,128)S(1)}, f32[40,2048]{1,0:T(8,128)}, u32[]{:S(2)}) copy-start(f32[40,2048]{1,0:T(8,128)} %get-tuple-element.20) | copy-start | bytes 983044
  180.4 84.4 %copy-start.6 = (f32[40,2048]{1,0:T(8,128)S(1)}, f32[40,2048]{1,0:T(8,128)}, u32[]{:S(2)}) copy-start(f32[40,2048]{1,0:T(8,128)} %get-tuple-element.22) | copy-start | bytes 983044
  180.4 85.3 %copy-start.4 = (f32[40,2048]{1,0:T(8,128)S(1)}, f32[40,2048]{1,0:T(8,128)}, u32[]{:S(2)}) copy-start(f32[40,2048]{1,0:T(8,128)} %get-tuple-element.21) | copy-start | bytes 983044
  180.9 84.9 %copy-start.2 = (f32[40,2048]{1,0:T(8,128)S(1)}, f32[40,2048]{1,0:T(8,128)}, u32[]{:S(2)}) copy-start(f32[40,2048]{1,0:T(8,128)} %get-tuple-element.23) | copy-start | bytes 983044
  251.4 15.4 %collective-permute-start.13 = (f32[40,128]{1,0:T(8,128)}, f32[40,128]{1,0:T(8,128)}, u32[]{:S(2)}, u32[]{:S(2)}) collective-permute-start(f32[40,128]{1,0:T(8,128)} %get-tuple-element.76), channel_id=1, source_target_pairs={{2,0},{3,1},{4,2},{5,3},{6,4},{7,5},{8,6},{9,7},{10,8},{11,9},{12,... | collective-permute-start | bytes 61448 | tf_op jit(solution)/shard_map/ppermute | solution.py:19
  255.6 11.2 %collective-permute-start.14 = (f32[40,128]{1,0:T(8,128)}, f32[40,128]{1,0:T(8,128)}, u32[]{:S(2)}, u32[]{:S(2)}) collective-permute-start(f32[40,128]{1,0:T(8,128)} %get-tuple-element.75), channel_id=1, source_target_pairs={{3,0},{4,1},{5,2},{6,3},{7,4},{8,5},{9,6},{10,7},{11,8},{12,9},{13... | collective-permute-start | bytes 61448 | tf_op jit(solution)/shard_map/ppermute | solution.py:19
  259.2 7.6 %collective-permute-start.15 = (f32[40,128]{1,0:T(8,128)}, f32[40,128]{1,0:T(8,128)}, u32[]{:S(2)}, u32[]{:S(2)}) collective-permute-start(f32[40,128]{1,0:T(8,128)} %get-tuple-element.74), channel_id=1, source_target_pairs={{4,0},{5,1},{6,2},{7,3},{8,4},{9,5},{10,6},{11,7},{12,8},{13,9},{1... | collective-permute-start | bytes 61448 | tf_op jit(solution)/shard_map/ppermute | solution.py:19
  269.2 4.0 %copy-start.66 = (s32[8192]{0:T(1024)S(1)}, s32[8192]{0:T(1024)}, u32[]{:S(2)}) copy-start(s32[8192]{0:T(1024)} %copy-done.65) | copy-start | bytes 98308
  273.2 30.0 %copy-start.100 = (pred[8192]{0:T(1024)(128)(4,1)S(1)}, pred[8192]{0:T(1024)(128)(4,1)}, u32[]{:S(2)}) copy-start(pred[8192]{0:T(1024)(128)(4,1)} %compare_and_fusion) | copy-start | bytes 24580
  315.8 6.6 %copy-start.102 = (pred[1,16,4,128]{3,1,2,0:T(8,128)(4,1)S(1)}, pred[1,16,4,128]{3,1,2,0:T(8,128)(4,1)}, u32[]{:S(2)}) copy-start(pred[1,16,4,128]{3,1,2,0:T(8,128)(4,1)} %copy.267) | copy-start | bytes 24580
  315.8 6.6 %copy-start.104 = (pred[1,16,4,128]{3,1,2,0:T(8,128)(4,1)S(1)}, pred[1,16,4,128]{3,1,2,0:T(8,128)(4,1)}, u32[]{:S(2)}) copy-start(pred[1,16,4,128]{3,1,2,0:T(8,128)(4,1)} %copy.270) | copy-start | bytes 24580
  (73 other events, 142.9 us)
where the time goes:
time: 336 us; the launch traced here: 332 us
  local copies, waits for them, and re-layouts  151 us (45%)
  blocking collectives  68.8 us (20%)
  starting transfers between devices  55.2 us (16%)
  other arithmetic  32.4 us (10%)
  matrix products  21.5 us (6%)
    psum x1, blocking collectives, local(): absorbed.append(lax.psum(totals, 'dom') * norm_factor)  68.8 us
    gather x2, local copies, waits for them, and re-layouts, local(): jnp.take(trace_table, gather_index, axis=1).reshape(4, 10, face_count)  60.1 us
    ppermute x16, starting transfers between devices, passed_along(): return lax.ppermute(value, axis, pairs)  55.2 us
    select_n x2, other arithmetic, local(): jnp.take(trace_table, gather_index, axis=1).reshape(4, 10, face_count)  14.9 us
    dot_general x2, matrix products, orient_values(): jnp.einsum('tnk,fkx->tfnx', rotate_tables, values, precision=lax.Precisio...  12.4 us
    gather x4, local copies, waits for them, and re-layouts, local(): jnp.take(flat_inner, send_index, axis=1)  10.3 us
    slice x2, local copies, waits for them, and re-layouts, face_flux(): inner_trace[1]  8.77 us
    unnamed x257, local copies, waits for them, and re-layouts  8.29 us
  transfers between devices with their start and end apart: 16, of which 0 were waited for; matrix products, arithmetic and copies ran while one was open for 11% of the time, Pallas kernels for 0%

commit v1 on v0

v1 whole, which is shorter than its diff:
```python
import functools
import math

import jax
import jax.numpy as jnp
import numpy as np
from jax import lax
from jax.experimental import pallas as pl
from jax.experimental.pallas import tpu as pltpu
from jax.sharding import PartitionSpec as P

NMAT = 16
NODES = 20
LANES = 128

section_decay = (-567301805773.0 / 1357537059087.0, -2404267990393.0 / 2016746695238.0)
section_weight = (1720146321549.0 / 2090206949498.0, 3134564353537.0 / 4481467310338.0)
time_step = 0.002


def mat_product(left, right):
    inner = len(right)
    return [
        [sum((left[i][k] * right[k][j] for k in range(inner))) for j in range(len(right[0]))]
        for i in range(len(left))
    ]


def flipped(matrix):
    return [list(row) for row in zip(*matrix)]


def solve_rows(matrix, right):
    size = len(matrix)
    augmented = [list(matrix[i]) + list(right[i]) for i in range(size)]
    for column in range(size):
        pivot = max(range(column, size), key=lambda r: abs(augmented[r][column]))
        augmented[column], augmented[pivot] = (augmented[pivot], augmented[column])
        leader = augmented[column][column]
        augmented[column] = [value / leader for value in augmented[column]]
        for other in range(size):
            if other != column:
                factor = augmented[other][column]
                if factor != 0.0:
                    augmented[other] = [
                        a - factor * b for a, b in zip(augmented[other], augmented[column])
                    ]
    return [row[size:] for row in augmented]


def identity_rows(size):
    return [[1.0 if i == j else 0.0 for j in range(size)] for i in range(size)]


def dg_tables():
    lattice = [(i, j, k) for i in range(4) for j in range(4 - i) for k in range(4 - i - j)]
    coords = [(i / 3.0, j / 3.0, k / 3.0) for i, j, k in lattice]
    vander = [[x**a * y**b * z**c for a, b, c in lattice] for x, y, z in coords]
    inverse = solve_rows(vander, identity_rows(20))
    gradient_rows = []
    for d in range(3):
        derived = []
        for point in coords:
            row = []
            for powers in lattice:
                if powers[d] == 0:
                    row.append(0.0)
                else:
                    lowered = [powers[0], powers[1], powers[2]]
                    lowered[d] = lowered[d] - 1
                    row.append(
                        powers[d]
                        * point[0] ** lowered[0]
                        * point[1] ** lowered[1]
                        * point[2] ** lowered[2]
                    )
            derived.append(row)
        gradient_rows.extend(mat_product(derived, inverse))
    mono_mass = [
        [
            math.factorial(a + p)
            * math.factorial(b + q)
            * math.factorial(c + r)
            / math.factorial(a + b + c + p + q + r + 3)
            for p, q, r in lattice
        ]
        for a, b, c in lattice
    ]
    mass_matrix = mat_product(mat_product(flipped(inverse), mono_mass), inverse)
    plane_points = [(a, b) for a in range(4) for b in range(4 - a)]
    face_coords = [(a / 3.0, b / 3.0) for a, b in plane_points]
    vander_face = [[x**a * y**b for a, b in plane_points] for x, y in face_coords]
    inverse_face = solve_rows(vander_face, identity_rows(10))
    mono_face = [
        [
            math.factorial(a + p) * math.factorial(b + q) / math.factorial(a + b + p + q + 2)
            for p, q in plane_points
        ]
        for a, b in plane_points
    ]
    face_mass = mat_product(mat_product(flipped(inverse_face), mono_face), inverse_face)
    position = {point: n for n, point in enumerate(lattice)}
    builders = [
        lambda a, b: (a, b, 0),
        lambda a, b: (a, 0, b),
        lambda a, b: (0, a, b),
        lambda a, b: (a, b, 3 - a - b),
    ]
    face_nodes = [[position[builder(a, b)] for a, b in plane_points] for builder in builders]
    surface = [[0.0] * 40 for n in range(20)]
    for f in range(4):
        for n in range(10):
            for m in range(10):
                surface[face_nodes[f][n]][f * 10 + m] = face_mass[n][m]
    lift_matrix = solve_rows(mass_matrix, surface)
    rotations = []
    for t in range(3):
        mapping = []
        for a, b in plane_points:
            triple = (b, a, 3 - a - b)
            for s in range(t):
                triple = (triple[1], triple[2], triple[0])
            mapping.append(plane_points.index((triple[0], triple[1])))
        rotations.append(mapping)
    return (gradient_rows, lift_matrix, face_nodes, rotations)


def peer_offsets(half_span):
    return [j - half_span if j < half_span else j - half_span + 1 for j in range(2 * half_span)]


VMEM = pl.BlockSpec(memory_space=pltpu.VMEM)
SMEM = pl.BlockSpec(memory_space=pltpu.SMEM)
F32 = jnp.float32
GRAD_ROWS, LIFT_ROWS, FACE_NODES, ROTATIONS = dg_tables()
TILES = [(0, 8), (8, 8), (16, 4)]


def lanes_of(c):
    return pl.ds(pl.multiple_of(c * LANES, LANES), LANES)


def rows_of(c):
    return pl.ds(pl.multiple_of(c * 8, 8), 8)


def lookup(row, lane_index):
    wide = jnp.broadcast_to(row, (8, LANES))
    return jnp.take_along_axis(wide, lane_index, axis=1, mode="promise_in_bounds")


def split_bf16(x):
    high = x.astype(jnp.bfloat16)
    low = (x - high.astype(F32)).astype(jnp.bfloat16)
    return high, low


def mm(a, b):
    return jnp.dot(a, b, preferred_element_type=F32)


def faces_to_rows(src, scratch, dst, convert):
    chunks = src.shape[1] // LANES
    for c in range(chunks):
        scratch[c * 8 : c * 8 + 4, :] = src[:, c * LANES : (c + 1) * LANES]
    for f in range(4):
        for part in range(chunks // 8):
            got = scratch[pl.ds(part * 64 + f, 8, stride=8), :]
            row = f * chunks + part * 8
            dst[row : row + 8, :] = convert(got)


def wave_tiles(fields, c, normals, face_acc, press_acc):
    for r, (_, size) in enumerate(TILES):
        press, vel = fields[0][r], [fields[i][r] for i in (1, 2, 3)]
        press_acc[r, pl.ds(pl.multiple_of(c * 8, 8), size), :] = press
        for f in range(4):
            wave = press
            for i in range(3):
                wave = wave + normals[i, f : f + 1, lanes_of(c)] * vel[i]
            face_acc[f, r, pl.ds(pl.multiple_of(c * 8, 8), size), :] = wave


def send_and_totals(chunks, section, face_acc, press_acc, link, refl, half_scale, mat, send_faces, totals_in, g, d, buf):
    losses, keys = [], []
    for f in range(4):
        for part in range(chunks // 8):
            row = f * chunks + part * 8
            squares = jnp.zeros((8, LANES), F32)
            for n in range(10):
                node = FACE_NODES[f][n]
                at = pl.ds(part * 64 + node % 8, 8, stride=8)
                wave = face_acc[f, node // 8, at, :]
                g[n, row : row + 8, :] = wave
                d[n, row : row + 8, :] = wave - 2.0 * press_acc[node // 8, at, :]
                squares = squares + wave * wave
            r = refl[row : row + 8, :]
            loss = 0.5 * half_scale[row : row + 8, :] * (1.0 - r * r) * squares
            losses.append(jnp.where(link[row : row + 8, :] < 0, loss, 0.0))
            keys.append(mat[row : row + 8, :])
    lane = lax.broadcasted_iota(jnp.int32, (1, LANES), 1)
    totals = totals_in
    for m in range(NMAT):
        total = jnp.zeros((8, LANES), F32)
        for loss, key in zip(losses, keys):
            total = total + jnp.where(key == m, loss, 0.0)
        one = jnp.sum(jnp.sum(total, axis=0, keepdims=True), axis=1, keepdims=True)
        totals = jnp.where(lane == section * NMAT + m, one, totals)

    sends = send_faces[...]
    low = sends & (LANES - 1)
    high = lax.shift_right_arithmetic(sends, 7)
    acc = [jnp.zeros((8, LANES), F32) for _ in range(10)]
    for h in range(4 * chunks):
        here = high == h
        for n in range(10):
            acc[n] = jnp.where(here, lookup(g[n, h : h + 1, :], low), acc[n])
    me = lax.axis_index("dom")
    count = buf.shape[0]

    def put(i, carry):
        buf[i, :, 10 * LANES : 11 * LANES] = totals
        return carry

    lax.fori_loop(0, count, put, 0, unroll=8)
    for j, offset in enumerate(peer_offsets(4)):
        there = me + offset

        @pl.when((there >= 0) & (there < count))
        def _():
            for n in range(10):
                buf[there, :, n * LANES : (n + 1) * LANES] = acc[n][j : j + 1, :]

    return totals


def first_kernel(sol, normals, neighbour, orientation, material, scale, impedance, send_faces, g, d, buf, link, orient, half_scale, refl, mat, totals, face_acc, press_acc, tmp, tmp_int):
    chunks = sol.shape[2] // LANES
    faces_to_rows(neighbour, tmp_int, link, lambda x: x)
    faces_to_rows(orientation, tmp_int, orient, lambda x: x)
    faces_to_rows(scale, tmp, half_scale, lambda x: 0.5 * x)
    faces_to_rows(material, tmp_int, mat, lambda x: x)
    for row in range(0, 4 * chunks, 8):
        key = mat[row : row + 8, :]
        picked = jnp.zeros((8, LANES), F32)
        for m in range(NMAT):
            picked = jnp.where(key == m, impedance[m], picked)
        refl[row : row + 8, :] = (picked - 1.0) / (picked + 1.0)

    def chunk(c, carry):
        fields = [[sol[i, at : at + size, lanes_of(c)] for at, size in TILES] for i in range(4)]
        wave_tiles(fields, c, normals, face_acc, press_acc)
        return carry

    lax.fori_loop(0, chunks, chunk, 0, unroll=2)
    totals[...] = send_and_totals(chunks, 0, face_acc, press_acc, link, refl, half_scale, mat, send_faces, jnp.zeros((1, LANES), F32), g, d, buf)


def local_kernel(decay, sol, reg, geometry, link, g, grad, out_g, out_reg):
    chunks = sol.shape[2] // LANES
    wide = 2 * LANES

    def volume(b, carry):
        at = pl.ds(pl.multiple_of(b * wide, wide), wide)
        vel = [sol[i, :, at] for i in (1, 2, 3)]
        press = split_bf16(sol[0, :, at])
        metric = [geometry[k : k + 1, at] for k in range(9)]
        div = None
        slopes = []
        for a in range(3):
            matrix = grad[a]
            flow = split_bf16(metric[a] * vel[0] + metric[3 + a] * vel[1] + metric[6 + a] * vel[2])
            term = mm(matrix, flow[0]) + mm(matrix, flow[1])
            div = term if div is None else div + term
            slopes.append(mm(matrix, press[0]) + mm(matrix, press[1]))
        out_reg[0, :, at] = decay * reg[0, :, at] - time_step * div
        for i in range(3):
            slope = metric[3 * i] * slopes[0] + metric[3 * i + 1] * slopes[1] + metric[3 * i + 2] * slopes[2]
            out_reg[1 + i, :, at] = decay * reg[1 + i, :, at] - time_step * slope
        return carry

    lax.fori_loop(0, chunks // 2, volume, 0)

    def group(j, carry):
        codes = link[rows_of(j), :]
        low = codes & (LANES - 1)
        high = lax.shift_right_arithmetic(codes, 7)
        acc = [jnp.zeros((8, LANES), F32) for _ in range(10)]
        for h in range(4 * chunks):
            here = high == h
            for n in range(10):
                acc[n] = jnp.where(here, lookup(g[n, h : h + 1, :], low), acc[n])
        for n in range(10):
            out_g[n, rows_of(j), :] = acc[n]
        return carry

    lax.fori_loop(0, 4 * chunks // 8, group, 0)


def finish(section, chunks, sol, normals, link, orient, half_scale, refl, g, d, outer, recv, reg_part, lift_high, lift_low, new_sol, new_reg, flux_acc, after):
    me = lax.axis_index("dom")
    count = recv.shape[0]
    local_faces = 4 * chunks
    peers = [jnp.clip(me + offset, 0, count - 1) for offset in peer_offsets(4)]
    for f in range(4):

        def group(part, carry, f=f):
            rows = pl.ds(pl.multiple_of(f * chunks + part * 8, 8), 8)
            codes = link[rows, :]
            low = codes & (LANES - 1)
            high = lax.shift_right_arithmetic(codes, 7)
            acc = [outer[n, rows, :] for n in range(10)]
            for j in range(8):
                here = high == local_faces + j
                for n in range(10):
                    row = recv[peers[j], :, n * LANES : (n + 1) * LANES]
                    acc[n] = jnp.where(here, lookup(row, low), acc[n])
            turn = orient[rows, :]
            wall = codes < 0
            r = refl[rows, :]
            scale = half_scale[rows, :]
            for n in range(10):
                a, b, c = (ROTATIONS[t][n] for t in range(3))
                turned = acc[a] if a == b == c else jnp.where(turn == 0, acc[a], jnp.where(turn == 1, acc[b], acc[c]))
                turned = jnp.where(wall, r * g[n, rows, :], turned)
                k = f * 10 + n
                at = pl.ds(part * 64 + k % 8, 8, stride=8)
                flux_acc[k // 8, at, :] = scale * (d[n, rows, :] + turned)
            return carry

        lax.fori_loop(0, chunks // 8, group, 0)

    weight = section_weight[section]

    def chunk(c, carry):
        at = lanes_of(c)
        flux = split_bf16(jnp.concatenate([flux_acc[k, rows_of(c), :] for k in range(5)], axis=0))
        lifted = mm(lift_high[...], flux[0]) + mm(lift_high[...], flux[1]) + mm(lift_low[...], flux[0])
        fields = [[], [], [], []]
        for start, size in TILES:
            pieces = [lifted[24 * f + start : 24 * f + start + size, :] for f in range(4)]
            for i in range(4):
                if i == 0:
                    total = pieces[0] + pieces[1] + pieces[2] + pieces[3]
                else:
                    total = None
                    for f in range(4):
                        term = normals[i - 1, f : f + 1, at] * pieces[f]
                        total = term if total is None else total + term
                    total = -total
                reg = reg_part[i, start : start + size, at] + time_step * total
                value = sol[i, start : start + size, at] + weight * reg
                new_reg[i, start : start + size, at] = reg
                new_sol[i, start : start + size, at] = value
                fields[i].append(value)
        after(c, fields)
        return carry

    lax.fori_loop(0, chunks, chunk, 0, unroll=2)


def middle_kernel(sol, normals, link, orient, half_scale, refl, mat, send_faces, g, d, outer, recv, reg_part, lift_high, lift_low, totals_in, new_sol, new_reg, new_g, new_d, buf, flux_acc, face_acc, press_acc):
    chunks = sol.shape[2] // LANES

    def after(c, fields):
        wave_tiles(fields, c, normals, face_acc, press_acc)

    finish(0, chunks, sol, normals, link, orient, half_scale, refl, g, d, outer, recv, reg_part, lift_high, lift_low, new_sol, new_reg, flux_acc, after)
    send_and_totals(chunks, 1, face_acc, press_acc, link, refl, half_scale, mat, send_faces, totals_in[...], new_g, new_d, buf)


def last_kernel(norm_factor, sol, normals, link, orient, half_scale, refl, g, d, outer, recv, reg_part, lift_high, lift_low, new_sol, new_reg, absorbed, flux_acc):
    chunks = sol.shape[2] // LANES
    finish(1, chunks, sol, normals, link, orient, half_scale, refl, g, d, outer, recv, reg_part, lift_high, lift_low, new_sol, new_reg, flux_acc, lambda c, fields: None)
    total = recv[0, :, 10 * LANES : 11 * LANES]
    for i in range(1, recv.shape[0]):
        total = total + recv[i, :, 10 * LANES : 11 * LANES]
    total = total * norm_factor
    absorbed[0:1, :] = total[:, 0:NMAT]
    absorbed[1:2, :] = total[:, NMAT : 2 * NMAT]


def local(solution, register, geometry, normals, face_scale, impedance, neighbour, orientation, wall_material, send_faces):
    elems = solution.shape[2]
    chunks = elems // LANES
    devices = lax.axis_size("dom")
    rows = 4 * chunks
    shape = jax.ShapeDtypeStruct
    lift = np.zeros((96, 40), np.float64)
    for f in range(4):
        for n in range(NODES):
            lift[24 * f + n, 10 * f : 10 * f + 10] = LIFT_ROWS[n][10 * f : 10 * f + 10]
    lift_high = lift.astype(jnp.bfloat16)
    lift_low = (lift - lift_high.astype(np.float64)).astype(jnp.bfloat16)
    lift_high, lift_low = jnp.asarray(lift_high), jnp.asarray(lift_low)
    grad = jnp.asarray(np.array(GRAD_ROWS).reshape(3, NODES, NODES), jnp.bfloat16)
    state = shape(solution.shape, F32)
    wave = shape((10, rows, LANES), F32)
    packet = shape((devices, 1, 11 * LANES), F32)
    plane = shape((rows, LANES), F32)
    plane_int = shape((rows, LANES), jnp.int32)
    line = shape((1, LANES), F32)
    face_scratch = pltpu.VMEM((4, 3, 8 * chunks, LANES), F32)
    press_scratch = pltpu.VMEM((3, 8 * chunks, LANES), F32)
    flux_scratch = pltpu.VMEM((5, 8 * chunks, LANES), F32)

    def call(body, args, specs, outs, scratch, name, flops=2_000_000):
        return pl.pallas_call(
            body,
            out_shape=outs,
            in_specs=specs,
            out_specs=jax.tree.map(lambda _: VMEM, outs),
            scratch_shapes=scratch,
            cost_estimate=pl.CostEstimate(flops=flops, bytes_accessed=4_000_000, transcendentals=0),
            name=name,
        )(*args)

    g, d, buf, link, orient, half_scale, refl, mat, totals = call(
        first_kernel,
        (solution, normals, neighbour, orientation, wall_material, face_scale, impedance, send_faces),
        [VMEM] * 6 + [SMEM, VMEM],
        (wave, wave, packet, plane_int, plane_int, plane, plane, plane_int, line),
        [face_scratch, press_scratch, pltpu.VMEM((8 * chunks, LANES), F32), pltpu.VMEM((8 * chunks, LANES), jnp.int32)],
        "first",
    )

    def inner(section, sol, reg, g):
        return call(
            functools.partial(local_kernel, section_decay[section]),
            (sol, reg, geometry, link, g, grad),
            [VMEM] * 6,
            (wave, state),
            [],
            "inner",
            20_000_000,
        )

    recv = lax.all_to_all(buf, "dom", 0, 0)
    outer, reg_part = inner(0, solution, register, g)
    sol, reg, g, d, buf = call(
        middle_kernel,
        (solution, normals, link, orient, half_scale, refl, mat, send_faces, g, d, outer, recv, reg_part, lift_high, lift_low, totals),
        [VMEM] * 16,
        (state, state, wave, wave, packet),
        [flux_scratch, face_scratch, press_scratch],
        "middle",
    )
    recv = lax.all_to_all(buf, "dom", 0, 0)
    outer, reg_part = inner(1, sol, reg, g)
    sol, reg, absorbed = call(
        functools.partial(last_kernel, NMAT / (devices * elems)),
        (sol, normals, link, orient, half_scale, refl, g, d, outer, recv, reg_part, lift_high, lift_low),
        [VMEM] * 13,
        (state, state, shape((2, NMAT), F32)),
        [flux_scratch],
        "last",
    )
    return sol, reg, absorbed


def solution(mesh):
    in_specs = (
        P(None, None, "dom"),
        P(None, None, "dom"),
        P(None, "dom"),
        P(None, None, "dom"),
        P(None, "dom"),
        P(),
        P(None, "dom"),
        P(None, "dom"),
        P(None, "dom"),
        P("dom", None),
    )
    out_specs = (P(None, None, "dom"), P(None, None, "dom"), P())
    return jax.shard_map(local, mesh=mesh, in_specs=in_specs, out_specs=out_specs, check_vma=False)
```

time: 336 us -> 75.2 us (0.22)
  the two profiles are of different devices: /device:TPU:33 before, /device:TPU:1 now
where the time goes in v1:
time: 75.2 us; the launch traced here: 74.8 us
  Pallas kernels  38 us (51%)
  starting transfers between devices  16.8 us (22%)
  waiting for transfers between devices  10.2 us (14%)
  local copies, waits for them, and re-layouts  9.12 us (12%)
    pallas_call x5, Pallas kernels, call(): pl.pallas_call(body, out_shape=outs, in_specs=specs, out_specs=jax.tree.m...  38 us
    all_to_all x2, starting transfers between devices, local(): recv = lax.all_to_all(buf, 'dom', 0, 0)  16.8 us
    all_to_all x2, waiting for transfers between devices, local(): recv = lax.all_to_all(buf, 'dom', 0, 0)  10.2 us
    unnamed x10, local copies, waits for them, and re-layouts  5.39 us
    pallas_call x2, local copies, waits for them, and re-layouts, call(): pl.pallas_call(body, out_shape=outs, in_specs=specs, out_specs=jax.tree.m...  3.73 us
  transfers between devices with their start and end apart: 2, of which 2 were waited for; matrix products, arithmetic and copies ran while one was open for 2% of the time, Pallas kernels for 27%

profile of v1, /device:TPU:1, one launch (start us, length us, event | category | flops | bytes accessed | tf_op | source)
XLA Modules:
  0.0 74.8 jit_solution(1283555482883360795)
XLA Ops:
  0.6 2.4 %copy.19.sol = f32[4,20,2048]{2,1,0:T(8,128)} copy(f32[4,20,2048]{2,0,1:T(4,128)} %param.13) | data formatting | bytes 1310720 | tf_op args[0]
  3.0 3.9 %first.1 = (f32[10,64,128]{2,1,0:T(8,128)}, f32[10,64,128]{2,1,0:T(8,128)}, f32[128,1,1408]{2,1,0:T(1,128)}, s32[64,128]{1,0:T(8,128)}, s32[64,128]{1,0:T(8,128)...) custom-call(f32[4,20,2048]{2,1,0:T(8,128)} %copy.19.sol, ...), custom_call_target="tpu_custom_call" | custom-call | flops 2000000 | bytes 4000000 | tf_op jit(solution)/shard_map/first/pallas_call | solution.py:408
  6.9 0.0 copy-start.3
  6.9 11.5 %all-to-all-start = ((f32[128,1,1408]{2,1,0:T(1,128)}), f32[128,1,1408]{2,1,0:T(1,128)S(1)}, u32[]{:S(2)}, u32[]{:S(2)}) async-start(f32[128,1,1408]{2,1,0:T(1,128)} %get-tuple-element.29), calls=%async_computation | async-start | bytes 1441792 | tf_op jit(solution)/shard_map/all_to_all | solution.py:438
  18.4 0.0 copy-done.3
  18.4 1.3 %copy.18.reg = f32[4,20,2048]{2,1,0:T(8,128)} copy(f32[4,20,2048]{2,0,1:T(4,128)S(1)} %copy-done.3) | data formatting | bytes 1310720 | tf_op args[1]
  19.7 10.0 %inner.2 = (f32[10,64,128]{2,1,0:T(8,128)}, f32[4,20,2048]{2,1,0:T(8,128)}) custom-call(f32[4,20,2048]{2,1,0:T(8,128)} %copy.19.sol, f32[4,20,2048]{2,1,0:T(8,128)} %copy.18.reg, f32[9,2048]{1,0:T(8,128)} %geometry.3, s32[64,128]{1,0:T(8,128)} %get-tuple-element.21.link, f32[10,64,128]{2,1,0:T(8,128)} %get-tuple-element.26.g, ...), custom_call_target="tpu_custom_call" | custom-call | flops 20000000 | bytes 4000000 | tf_op jit(solution)/shard_map/inner/pallas_call | solution.py:408
  29.7 4.4 %all-to-all-done.recv = f32[128,1,1408]{2,1,0:T(1,128)S(1)} async-done(((f32[128,1,1408]{2,1,0:T(1,128)}), f32[128,1,1408]{2,1,0:T(1,128)S(1)}, u32[]{:S(2)}, u32[]{:S(2)}) %all-to-all-start) | async-done | bytes 720928 | tf_op jit(solution)/shard_map/all_to_all | solution.py:438
  34.1 0.0 copy-start.1
  34.1 0.9 %copy-done.1 = f32[128,1,1408]{2,1,0:T(1,128)} copy-done((f32[128,1,1408]{2,1,0:T(1,128)}, f32[128,1,1408]{2,1,0:T(1,128)S(1)}, u32[]{:S(2)}) %copy-start.1) | copy-done | bytes 720920
  35.0 8.0 %middle.1 = (f32[4,20,2048]{2,1,0:T(8,128)}, f32[4,20,2048]{2,1,0:T(8,128)}, f32[10,64,128]{2,1,0:T(8,128)}, f32[10,64,128]{2,1,0:T(8,128)}, f32[128,1,1408]{2,1,0:T(1,128)}) custom-call(f32[4,20,2048]{2,1,0:T(8,128)} %copy.19.sol, f32[3,4,2048]{2,1,0:T(4,128)} %normals.5, s32[64,128]{1,0:T(8,128)} %get-tuple-element.21.link, ...), custom_call_target="tpu_custom_call" | custom-call | flops 2000000 | bytes 4000000 | tf_op jit(solution)/shard_map/middle/pallas_call | solution.py:408
  43.0 5.3 %all-to-all-start.1 = ((f32[128,1,1408]{2,1,0:T(1,128)}), f32[128,1,1408]{2,1,0:T(1,128)S(1)}, u32[]{:S(2)}, u32[]{:S(2)}) async-start(f32[128,1,1408]{2,1,0:T(1,128)} %get-tuple-element.37), calls=%async_computation.1 | async-start | bytes 1441792 | tf_op jit(solution)/shard_map/all_to_all | solution.py:448
  48.3 10.0 %inner.3 = (f32[10,64,128]{2,1,0:T(8,128)}, f32[4,20,2048]{2,1,0:T(8,128)}) custom-call(f32[4,20,2048]{2,1,0:T(8,128)} %get-tuple-element.32.sol, f32[4,20,2048]{2,1,0:T(8,128)} %get-tuple-element.35.reg, f32[9,2048]{1,0:T(8,128)} %geometry.3, s32[64,128]{1,0:T(8,128)} %get-tuple-element.21.link, f32[10,64,128]{2,1,0:T(8,128)} %get-tuple-element.33.g, ...), custom_call_target="tpu_custom_call" | custom-call | flops 20000000 | bytes 4000000 | tf_op jit(solution)/shard_map/inner/pallas_call | solution.py:408
  58.3 5.7 %all-to-all-done.1.recv = f32[128,1,1408]{2,1,0:T(1,128)S(1)} async-done(((f32[128,1,1408]{2,1,0:T(1,128)}), f32[128,1,1408]{2,1,0:T(1,128)S(1)}, u32[]{:S(2)}, u32[]{:S(2)}) %all-to-all-start.1) | async-done | bytes 720928 | tf_op jit(solution)/shard_map/all_to_all | solution.py:448
  64.1 0.0 copy-start
  64.1 0.9 %copy-done = f32[128,1,1408]{2,1,0:T(1,128)} copy-done((f32[128,1,1408]{2,1,0:T(1,128)}, f32[128,1,1408]{2,1,0:T(1,128)S(1)}, u32[]{:S(2)}) %copy-start) | copy-done | bytes 720920
  64.9 6.2 %last.1 = (f32[4,20,2048]{2,1,0:T(8,128)}, f32[4,20,2048]{2,1,0:T(8,128)}, f32[2,16]{1,0:T(2,128)}) custom-call(f32[4,20,2048]{2,1,0:T(8,128)} %get-tuple-element.32.sol, f32[3,4,2048]{2,1,0:T(4,128)} %normals.5, s32[64,128]{1,0:T(8,128)} %get-tuple-element.21.link, s32[64,128]{1,0:T(8,128)} %get-tuple-element.22.orient, ...), custom_call_target="tpu_custom_call" | custom-call | flops 2000000 | bytes 4000000 | tf_op jit(solution)/shard_map/last/pallas_call | solution.py:408
  71.1 0.0 copy-start.2
  71.1 2.5 %copy.20 = f32[4,20,2048]{2,0,1:T(4,128)} copy(f32[4,20,2048]{2,1,0:T(8,128)} %get-tuple-element.39) | data formatting | bytes 1310720 | tf_op jit(solution)/shard_map/last/pallas_call | solution.py:408
  73.6 0.0 copy-done.2
  73.6 1.3 %copy.21 = f32[4,20,2048]{2,0,1:T(4,128)} copy(f32[4,20,2048]{2,1,0:T(8,128)S(1)} %copy-done.2) | data formatting | bytes 1310720 | tf_op jit(solution)/shard_map/last/pallas_call | solution.py:408
Async XLA Ops:
  6.9 11.5 %copy-start.3 = (f32[4,20,2048]{2,0,1:T(4,128)S(1)}, f32[4,20,2048]{2,0,1:T(4,128)}, u32[]{:S(2)}) copy-start(f32[4,20,2048]{2,0,1:T(4,128)} %param.14) | copy-start | bytes 1966084
  6.9 27.2 %all-to-all-start = ((f32[128,1,1408]{2,1,0:T(1,128)}), f32[128,1,1408]{2,1,0:T(1,128)S(1)}, u32[]{:S(2)}, u32[]{:S(2)}) async-start(f32[128,1,1408]{2,1,0:T(1,128)} %get-tuple-element.29), calls=%async_computation | async-start | bytes 1441792 | tf_op jit(solution)/shard_map/all_to_all | solution.py:438
  34.1 0.9 %copy-start.1 = (f32[128,1,1408]{2,1,0:T(1,128)}, f32[128,1,1408]{2,1,0:T(1,128)S(1)}, u32[]{:S(2)}) copy-start(f32[128,1,1408]{2,1,0:T(1,128)S(1)} %all-to-all-done.recv) | copy-start | bytes 2162692
  43.0 21.1 %all-to-all-start.1 = ((f32[128,1,1408]{2,1,0:T(1,128)}), f32[128,1,1408]{2,1,0:T(1,128)S(1)}, u32[]{:S(2)}, u32[]{:S(2)}) async-start(f32[128,1,1408]{2,1,0:T(1,128)} %get-tuple-element.37), calls=%async_computation.1 | async-start | bytes 1441792 | tf_op jit(solution)/shard_map/all_to_all | solution.py:448
  64.1 0.9 %copy-start = (f32[128,1,1408]{2,1,0:T(1,128)}, f32[128,1,1408]{2,1,0:T(1,128)S(1)}, u32[]{:S(2)}) copy-start(f32[128,1,1408]{2,1,0:T(1,128)S(1)} %all-to-all-done.1.recv) | copy-start | bytes 2162692
  71.1 2.5 %copy-start.2 = (f32[4,20,2048]{2,1,0:T(8,128)S(1)}, f32[4,20,2048]{2,1,0:T(8,128)}, u32[]{:S(2)}) copy-start(f32[4,20,2048]{2,1,0:T(8,128)} %get-tuple-element.40) | copy-start | bytes 1966084

commit v2 on v1

v2 whole, which is shorter than its diff:
```python
import functools
import math

import jax
import jax.numpy as jnp
import numpy as np
from jax import lax
from jax.experimental import pallas as pl
from jax.experimental.pallas import tpu as pltpu
from jax.sharding import PartitionSpec as P

NMAT = 16
NODES = 20
LANES = 128

section_decay = (-567301805773.0 / 1357537059087.0, -2404267990393.0 / 2016746695238.0)
section_weight = (1720146321549.0 / 2090206949498.0, 3134564353537.0 / 4481467310338.0)
time_step = 0.002


def mat_product(left, right):
    inner = len(right)
    return [
        [sum((left[i][k] * right[k][j] for k in range(inner))) for j in range(len(right[0]))]
        for i in range(len(left))
    ]


def flipped(matrix):
    return [list(row) for row in zip(*matrix)]


def solve_rows(matrix, right):
    size = len(matrix)
    augmented = [list(matrix[i]) + list(right[i]) for i in range(size)]
    for column in range(size):
        pivot = max(range(column, size), key=lambda r: abs(augmented[r][column]))
        augmented[column], augmented[pivot] = (augmented[pivot], augmented[column])
        leader = augmented[column][column]
        augmented[column] = [value / leader for value in augmented[column]]
        for other in range(size):
            if other != column:
                factor = augmented[other][column]
                if factor != 0.0:
                    augmented[other] = [
                        a - factor * b for a, b in zip(augmented[other], augmented[column])
                    ]
    return [row[size:] for row in augmented]


def identity_rows(size):
    return [[1.0 if i == j else 0.0 for j in range(size)] for i in range(size)]


def dg_tables():
    lattice = [(i, j, k) for i in range(4) for j in range(4 - i) for k in range(4 - i - j)]
    coords = [(i / 3.0, j / 3.0, k / 3.0) for i, j, k in lattice]
    vander = [[x**a * y**b * z**c for a, b, c in lattice] for x, y, z in coords]
    inverse = solve_rows(vander, identity_rows(20))
    gradient_rows = []
    for d in range(3):
        derived = []
        for point in coords:
            row = []
            for powers in lattice:
                if powers[d] == 0:
                    row.append(0.0)
                else:
                    lowered = [powers[0], powers[1], powers[2]]
                    lowered[d] = lowered[d] - 1
                    row.append(
                        powers[d]
                        * point[0] ** lowered[0]
                        * point[1] ** lowered[1]
                        * point[2] ** lowered[2]
                    )
            derived.append(row)
        gradient_rows.extend(mat_product(derived, inverse))
    mono_mass = [
        [
            math.factorial(a + p)
            * math.factorial(b + q)
            * math.factorial(c + r)
            / math.factorial(a + b + c + p + q + r + 3)
            for p, q, r in lattice
        ]
        for a, b, c in lattice
    ]
    mass_matrix = mat_product(mat_product(flipped(inverse), mono_mass), inverse)
    plane_points = [(a, b) for a in range(4) for b in range(4 - a)]
    face_coords = [(a / 3.0, b / 3.0) for a, b in plane_points]
    vander_face = [[x**a * y**b for a, b in plane_points] for x, y in face_coords]
    inverse_face = solve_rows(vander_face, identity_rows(10))
    mono_face = [
        [
            math.factorial(a + p) * math.factorial(b + q) / math.factorial(a + b + p + q + 2)
            for p, q in plane_points
        ]
        for a, b in plane_points
    ]
    face_mass = mat_product(mat_product(flipped(inverse_face), mono_face), inverse_face)
    position = {point: n for n, point in enumerate(lattice)}
    builders = [
        lambda a, b: (a, b, 0),
        lambda a, b: (a, 0, b),
        lambda a, b: (0, a, b),
        lambda a, b: (a, b, 3 - a - b),
    ]
    face_nodes = [[position[builder(a, b)] for a, b in plane_points] for builder in builders]
    surface = [[0.0] * 40 for n in range(20)]
    for f in range(4):
        for n in range(10):
            for m in range(10):
                surface[face_nodes[f][n]][f * 10 + m] = face_mass[n][m]
    lift_matrix = solve_rows(mass_matrix, surface)
    rotations = []
    for t in range(3):
        mapping = []
        for a, b in plane_points:
            triple = (b, a, 3 - a - b)
            for s in range(t):
                triple = (triple[1], triple[2], triple[0])
            mapping.append(plane_points.index((triple[0], triple[1])))
        rotations.append(mapping)
    return (gradient_rows, lift_matrix, face_nodes, rotations)


def peer_offsets(half_span):
    return [j - half_span if j < half_span else j - half_span + 1 for j in range(2 * half_span)]


VMEM = pl.BlockSpec(memory_space=pltpu.VMEM)
SMEM = pl.BlockSpec(memory_space=pltpu.SMEM)
F32 = jnp.float32
GRAD_ROWS, LIFT_ROWS, FACE_NODES, ROTATIONS = dg_tables()
LIFT_CHUNKS = 4
GRANT = None
BYTES = 4_000_000
TILES = [(0, 8), (8, 8), (16, 4)]


def lanes_of(c):
    return pl.ds(pl.multiple_of(c * LANES, LANES), LANES)


def rows_of(c):
    return pl.ds(pl.multiple_of(c * 8, 8), 8)


def lookup(row, lane_index):
    wide = jnp.broadcast_to(row, (8, LANES))
    return jnp.take_along_axis(wide, lane_index, axis=1, mode="promise_in_bounds")


def split_bf16(x):
    high = x.astype(jnp.bfloat16)
    low = (x - high.astype(F32)).astype(jnp.bfloat16)
    return high, low


def mm(a, b):
    return jnp.dot(a, b, preferred_element_type=F32)


class Staged:
    def __init__(self, outside, held, sems, count_in):
        self.outside, self.held, self.sems, self.count_in = outside, held, sems, count_in

    def copy(self, k):
        pair = (self.outside[k], self.held[k]) if k < self.count_in else (self.held[k], self.outside[k])
        return pltpu.make_async_copy(pair[0], pair[1], self.sems.at[k])


def staged(body, count_in, count_out, skip):
    total = count_in + count_out
    kept = [k for k in range(total) if k not in skip]

    def kernel(*refs):
        outside = refs[:total]
        held = list(outside)
        for at, k in enumerate(kept):
            held[k] = refs[total + at]
        rest = refs[total + len(kept) : -1]
        stage = Staged(outside, held, refs[-1], count_in)
        for k in kept:
            if k < count_in:
                stage.copy(k).start()
        waited, sent = set(), set()

        def wait(*names):
            for k in names:
                if k not in waited:
                    waited.add(k)
                    stage.copy(k).wait()

        def emit(*names):
            for k in names:
                sent.add(count_in + k)
                stage.copy(count_in + k).start()

        body(wait, emit, *held, *rest)
        wait(*[k for k in kept if k < count_in])
        emit(*[k - count_in for k in kept if k >= count_in and k not in sent])
        for k in kept:
            if k >= count_in:
                stage.copy(k).wait()

    return kernel, kept


def faces_to_rows(src, scratch, dst, convert):
    chunks = src.shape[1] // LANES
    for c in range(chunks):
        scratch[c * 8 : c * 8 + 4, :] = src[:, c * LANES : (c + 1) * LANES]
    for f in range(4):
        for part in range(chunks // 8):
            got = scratch[pl.ds(part * 64 + f, 8, stride=8), :]
            row = f * chunks + part * 8
            dst[row : row + 8, :] = convert(got)


def spread(src, dst, chunks):
    def chunk(c, carry):
        for node in range(NODES):
            dst[pl.ds(c * 24 + node, 4, stride=chunks * 24), :] = src[node, :, lanes_of(c)]
        return carry

    lax.fori_loop(0, chunks, chunk, 0, unroll=2)


def collect(src, dst, chunks):
    def chunk(c, carry):
        for node in range(NODES):
            dst[node, :, lanes_of(c)] = src[pl.ds(c * 24 + node, 4, stride=chunks * 24), :]
        return carry

    lax.fori_loop(0, chunks, chunk, 0, unroll=2)


def state_rows(field, c, chunks, start, size):
    return pl.ds(pl.multiple_of((field * chunks + c) * 24 + start, 8), size)


def wave_tiles(fields, c, chunks, normals, waves):
    for r, (start, size) in enumerate(TILES):
        press, vel = fields[0][r], [fields[i][r] for i in (1, 2, 3)]
        for f in range(4):
            wave = press
            for i in range(3):
                wave = wave + normals[i, f : f + 1, lanes_of(c)] * vel[i]
            waves[state_rows(f, c, chunks, start, size), :] = wave


def at_face(ref, field, chunks, part, node):
    return ref[pl.ds((field * chunks + part * 8) * 24 + node, 8, stride=24), :]


def pack(chunks, waves, send_faces, g, outgoing, filled):
    for f in range(4):
        for part in range(chunks // 8):
            row = f * chunks + part * 8
            for n in range(10):
                g[n, row : row + 8, :] = at_face(waves, f, chunks, part, FACE_NODES[f][n])
    filled()
    sends = send_faces[...]
    low = sends & (LANES - 1)
    high = lax.shift_right_arithmetic(sends, 7)
    acc = [jnp.zeros((8, LANES), F32) for _ in range(10)]
    for h in range(4 * chunks):
        here = high == h
        for n in range(10):
            acc[n] = jnp.where(here, lookup(g[n, h : h + 1, :], low), acc[n])
    for n in range(10):
        for j in range(8):
            outgoing[j, :, n * LANES : (n + 1) * LANES] = acc[n][j : j + 1, :]


def each_peer(count, act):
    me = lax.axis_index("dom")
    for j, offset in enumerate(peer_offsets(4)):
        there = me + offset

        @pl.when((there >= 0) & (there < count))
        def _():
            act(j, there)


def post(outgoing, buf, sems):
    def copy(j, there):
        return pltpu.make_async_copy(outgoing.at[j], buf.at[there, :, pl.ds(0, 10 * LANES)], sems.at[j])

    each_peer(buf.shape[0], lambda j, there: copy(j, there).start())
    return lambda: each_peer(buf.shape[0], lambda j, there: copy(j, there).wait())


def collect_blocks(recv, incoming, sems):
    def copy(j, there):
        return pltpu.make_async_copy(recv.at[there, :, pl.ds(0, 10 * LANES)], incoming.at[j], sems.at[j])

    each_peer(recv.shape[0], lambda j, there: copy(j, there).start())
    return lambda: each_peer(recv.shape[0], lambda j, there: copy(j, there).wait())


def wall_losses(section, chunks, g, link, refl, half_scale, mat, totals):
    losses, keys = [], []
    for row in range(0, 4 * chunks, 8):
        rows = slice(row, row + 8)
        squares = jnp.zeros((8, LANES), F32)
        for n in range(10):
            wave = g[n, rows, :]
            squares = squares + wave * wave
        r = refl[rows, :]
        losses.append(jnp.where(link[rows, :] < 0, 0.5 * half_scale[rows, :] * (1.0 - r * r) * squares, 0.0))
        keys.append(mat[rows, :])
    lane = lax.broadcasted_iota(jnp.int32, (1, LANES), 1)
    for m in range(NMAT):
        total = jnp.zeros((8, LANES), F32)
        for loss, key in zip(losses, keys):
            total = total + jnp.where(key == m, loss, 0.0)
        one = jnp.sum(jnp.sum(total, axis=0, keepdims=True), axis=1, keepdims=True)
        totals = jnp.where(lane == section * NMAT + m, one, totals)
    return totals


def first_kernel(wait, emit, sol, normals, send_faces, state, g, buf, waves, outgoing, sems):
    chunks = sol.shape[2] // LANES
    wait(0)
    spread(sol, state, chunks)
    emit(0)
    wait(1)

    def chunk(c, carry):
        fields = [[state[state_rows(i, c, chunks, start, size), :] for start, size in TILES] for i in range(4)]
        wave_tiles(fields, c, chunks, normals, waves)
        return carry

    lax.fori_loop(0, chunks, chunk, 0, unroll=2)
    wait(2)
    pack(chunks, waves, send_faces, g, outgoing, lambda: emit(1))
    post(outgoing, buf, sems)()


def inside(decay, chunks, state, reg, geometry, link, g, grad, out_g, out_reg):
    def volume(b, carry):
        def pair(ref, field):
            return jnp.concatenate([ref[state_rows(field, 2 * b + k, chunks, 0, NODES), :] for k in (0, 1)], axis=1)

        at = pl.ds(pl.multiple_of(b * 2 * LANES, 2 * LANES), 2 * LANES)
        vel = [pair(state, i) for i in (1, 2, 3)]
        press = split_bf16(pair(state, 0))
        metric = [geometry[k : k + 1, at] for k in range(9)]
        div = None
        slopes = []
        for a in range(3):
            matrix = grad[a]
            flow = split_bf16(metric[a] * vel[0] + metric[3 + a] * vel[1] + metric[6 + a] * vel[2])
            term = mm(matrix, flow[0]) + mm(matrix, flow[1])
            div = term if div is None else div + term
            slopes.append(mm(matrix, press[0]) + mm(matrix, press[1]))
        results = [div]
        for i in range(3):
            results.append(metric[3 * i] * slopes[0] + metric[3 * i + 1] * slopes[1] + metric[3 * i + 2] * slopes[2])
        for i in range(4):
            for k in (0, 1):
                rows = state_rows(i, 2 * b + k, chunks, 0, NODES)
                out_reg[rows, :] = decay * reg[rows, :] - time_step * results[i][:, k * LANES : (k + 1) * LANES]
        return carry

    lax.fori_loop(0, chunks // 2, volume, 0)

    def group(j, carry):
        codes = link[rows_of(j), :]
        low = codes & (LANES - 1)
        high = lax.shift_right_arithmetic(codes, 7)
        acc = [jnp.zeros((8, LANES), F32) for _ in range(10)]
        for h in range(4 * chunks):
            here = high == h
            for n in range(10):
                acc[n] = jnp.where(here, lookup(g[n, h : h + 1, :], low), acc[n])
        for n in range(10):
            out_g[n, rows_of(j), :] = acc[n]
        return carry

    lax.fori_loop(0, 4 * chunks // 8, group, 0)


def inner_first_kernel(wait, emit, state, reg, geometry, g, grad, neighbour, orientation, material, scale, impedance, out_g, out_reg, link, orient, half_scale, refl, mat, totals, reg_rows, tmp, tmp_int):
    chunks = neighbour.shape[1] // LANES
    wait(*range(9))
    faces_to_rows(neighbour, tmp_int, link, lambda x: x)
    faces_to_rows(orientation, tmp_int, orient, lambda x: x)
    faces_to_rows(scale, tmp, half_scale, lambda x: 0.5 * x)
    faces_to_rows(material, tmp_int, mat, lambda x: x)
    for row in range(0, 4 * chunks, 8):
        key = mat[row : row + 8, :]
        picked = jnp.zeros((8, LANES), F32)
        for m in range(NMAT):
            picked = jnp.where(key == m, impedance[m], picked)
        refl[row : row + 8, :] = (picked - 1.0) / (picked + 1.0)
    totals[...] = wall_losses(0, chunks, g, link, refl, half_scale, mat, jnp.zeros((1, LANES), F32))
    spread(reg, reg_rows, chunks)
    inside(section_decay[0], chunks, state, reg_rows, geometry, link, g, grad, out_g, out_reg)


def inner_second_kernel(wait, emit, state, reg, geometry, g, grad, link, out_g, out_reg):
    wait(*range(6))
    inside(section_decay[1], geometry.shape[1] // LANES, state, reg, geometry, link, g, grad, out_g, out_reg)


def finish(section, chunks, state, normals, link, orient, half_scale, refl, g, outer, incoming, reg_part, lift_high, lift_low, new_state, new_reg, flux_acc, lift_acc, ready, after):
    local_faces = 4 * chunks
    for f in range(4):
        for part in range(chunks // 8):
            row = f * chunks + part * 8
            rows = slice(row, row + 8)
            codes = link[rows, :]
            low = codes & (LANES - 1)
            high = lax.shift_right_arithmetic(codes, 7)
            acc = [outer[n, rows, :] for n in range(10)]
            for j in range(8):
                here = high == local_faces + j
                for n in range(10):
                    got = incoming[j, :, n * LANES : (n + 1) * LANES]
                    acc[n] = jnp.where(here, lookup(got, low), acc[n])
            turn = orient[rows, :]
            wall = codes < 0
            r = refl[rows, :]
            scale = half_scale[rows, :]
            for n in range(10):
                a, b, c = (ROTATIONS[t][n] for t in range(3))
                turned = acc[a] if a == b == c else jnp.where(turn == 0, acc[a], jnp.where(turn == 1, acc[b], acc[c]))
                own = g[n, rows, :]
                turned = own + jnp.where(wall, r * own, turned)
                press = at_face(state, 0, chunks, part, FACE_NODES[f][n])
                k = f * 10 + n
                flux_acc[k // 8, pl.ds(part * 64 + k % 8, 8, stride=8), :] = scale * (turned - 2.0 * press)

    for c in range(0, chunks, LIFT_CHUNKS):
        flux = split_bf16(
            jnp.concatenate(
                [jnp.concatenate([flux_acc[k, (c + b) * 8 : (c + b) * 8 + 8, :] for b in range(LIFT_CHUNKS)], axis=1) for k in range(5)],
                axis=0,
            )
        )
        lifted = mm(lift_high[...], flux[0]) + mm(lift_high[...], flux[1]) + mm(lift_low[...], flux[0])
        for b in range(LIFT_CHUNKS):
            lift_acc[c + b, :, :] = lifted[:, b * LANES : (b + 1) * LANES]

    weight = section_weight[section]
    ready()

    def chunk(c, carry):
        at = lanes_of(c)
        fields = [[], [], [], []]
        for start, size in TILES:
            pieces = [lift_acc[c, 24 * f + start : 24 * f + start + size, :] for f in range(4)]
            for i in range(4):
                if i == 0:
                    total = time_step * ((pieces[0] + pieces[1]) + (pieces[2] + pieces[3]))
                else:
                    terms = [normals[i - 1, f : f + 1, at] * pieces[f] for f in range(4)]
                    total = -time_step * ((terms[0] + terms[1]) + (terms[2] + terms[3]))
                rows = state_rows(i, c, chunks, start, size)
                reg = reg_part[rows, :] + total
                value = state[rows, :] + weight * reg
                new_reg[rows, :] = reg
                new_state[rows, :] = value
                fields[i].append(value)
        after(c, fields)
        return carry

    lax.fori_loop(0, chunks, chunk, 0, unroll=4)


def middle_kernel(wait, emit, state, normals, link, orient, half_scale, refl, mat, send_faces, g, outer, recv, reg_part, lift_high, lift_low, totals_in, new_state, new_reg, new_g, buf, flux_acc, lift_acc, waves, outgoing, incoming, losses, sems):
    chunks = normals.shape[2] // LANES
    arrived = collect_blocks(recv, incoming, sems)
    wait(0, 2, 3, 4, 5, 8, 9, 12, 13)
    arrived()

    def after(c, fields):
        wave_tiles(fields, c, chunks, normals, waves)

    finish(0, chunks, state, normals, link, orient, half_scale, refl, g, outer, incoming, reg_part, lift_high, lift_low, new_state, new_reg, flux_acc, lift_acc, lambda: wait(1, 11), after)
    emit(0, 1)
    wait(6, 7, 14)
    pack(chunks, waves, send_faces, new_g, outgoing, lambda: emit(2))
    posted = post(outgoing, buf, sems)
    totals = wall_losses(1, chunks, new_g, link, refl, half_scale, mat, totals_in[...])
    losses[...] = jnp.broadcast_to(totals, losses.shape)
    copy = pltpu.make_async_copy(losses, buf.at[:, 0, pl.ds(10 * LANES, LANES)], sems.at[8])
    copy.start()
    posted()
    copy.wait()


def last_kernel(norm_factor, wait, emit, state, normals, link, orient, half_scale, refl, g, outer, recv, reg_part, lift_high, lift_low, new_sol, new_reg, absorbed, flux_acc, lift_acc, sol_rows, reg_rows, incoming, losses, sems):
    chunks = normals.shape[2] // LANES
    arrived = collect_blocks(recv, incoming, sems)
    copy = pltpu.make_async_copy(recv.at[:, 0, pl.ds(10 * LANES, LANES)], losses, sems.at[8])
    copy.start()
    wait(0, 2, 3, 4, 5, 6, 7, 10, 11)
    arrived()
    finish(1, chunks, state, normals, link, orient, half_scale, refl, g, outer, incoming, reg_part, lift_high, lift_low, sol_rows, reg_rows, flux_acc, lift_acc, lambda: wait(1, 9), lambda c, fields: None)
    collect(reg_rows, new_reg, chunks)
    emit(1)
    collect(sol_rows, new_sol, chunks)
    emit(0)
    copy.wait()
    total = jnp.sum(losses[...], axis=0, keepdims=True) * norm_factor
    absorbed[0:1, :] = total[:, 0:NMAT]
    absorbed[1:2, :] = total[:, NMAT : 2 * NMAT]


def local(solution, register, geometry, normals, face_scale, impedance, neighbour, orientation, wall_material, send_faces):
    elems = solution.shape[2]
    chunks = elems // LANES
    devices = lax.axis_size("dom")
    rows = 4 * chunks
    shape = jax.ShapeDtypeStruct
    lift = np.zeros((96, 40), np.float64)
    for f in range(4):
        for n in range(NODES):
            lift[24 * f + n, 10 * f : 10 * f + 10] = LIFT_ROWS[n][10 * f : 10 * f + 10]
    lift_high = lift.astype(jnp.bfloat16)
    lift_low = (lift - lift_high.astype(np.float64)).astype(jnp.bfloat16)
    lift_high, lift_low = jnp.asarray(lift_high), jnp.asarray(lift_low)
    grad = jnp.asarray(np.array(GRAD_ROWS).reshape(3, NODES, NODES), jnp.bfloat16)
    swapped = shape((NODES, 4, elems), F32)
    state_shape = shape((4 * chunks * 24, LANES), F32)
    wave = shape((10, rows, LANES), F32)
    plane = shape((rows, LANES), F32)
    plane_int = shape((rows, LANES), jnp.int32)
    line = shape((1, LANES), F32)
    state_scratch = pltpu.VMEM((4 * chunks * 24, LANES), F32)
    flux_scratch = pltpu.VMEM((5, 8 * chunks, LANES), F32)
    lift_scratch = pltpu.VMEM((chunks, 96, LANES), F32)

    def packet(parts):
        return shape((devices, 1, parts * LANES), F32)

    def call(body, args, outs, scratch, name, flops=2_000_000, skip=()):
        total = len(args) + len(outs)
        skip = set(skip) | {k for k, a in enumerate(args) if a.ndim == 1}
        kernel, kept = staged(body, len(args), len(outs), skip)
        arrays = [*args, *outs]
        return pl.pallas_call(
            kernel,
            out_shape=outs,
            in_specs=[SMEM if a.ndim == 1 else pl.BlockSpec(memory_space=pl.ANY) for a in args],
            out_specs=tuple(pl.BlockSpec(memory_space=pl.ANY) for _ in outs),
            scratch_shapes=[pltpu.VMEM(arrays[k].shape, arrays[k].dtype) for k in kept]
            + scratch
            + [pltpu.SemaphoreType.DMA((total,))],
            compiler_params=pltpu.CompilerParams(vmem_limit_bytes=GRANT),
            cost_estimate=pl.CostEstimate(flops=flops, bytes_accessed=BYTES, transcendentals=0),
            name=name,
        )(*args)

    blocks = pltpu.VMEM((8, 1, 10 * LANES), F32)
    all_losses = pltpu.VMEM((devices, LANES), F32)
    sems = pltpu.SemaphoreType.DMA((9,))
    turned = solution.transpose(1, 0, 2)
    state, g, buf = call(first_kernel, (turned, normals, send_faces), (state_shape, wave, packet(10)), [state_scratch, blocks, sems], "first", skip=(5,))
    recv = pltpu.with_memory_space_constraint(lax.all_to_all(buf, "dom", 0, 0), pltpu.HBM)
    outer, reg_part, link, orient, half_scale, refl, mat, totals = call(
        inner_first_kernel,
        (state, register.transpose(1, 0, 2), geometry, g, grad, neighbour, orientation, wall_material, face_scale, impedance),
        (wave, state_shape, plane_int, plane_int, plane, plane, plane_int, line),
        [state_scratch, pltpu.VMEM((8 * chunks, LANES), F32), pltpu.VMEM((8 * chunks, LANES), jnp.int32)],
        "inner",
        20_000_000,
    )
    state, reg, g, buf = call(
        middle_kernel,
        (state, normals, link, orient, half_scale, refl, mat, send_faces, g, outer, recv, reg_part, lift_high, lift_low, totals),
        (state_shape, state_shape, wave, packet(11)),
        [flux_scratch, lift_scratch, state_scratch, blocks, blocks, all_losses, sems],
        "middle",
        skip=(10, 18),
    )
    recv = pltpu.with_memory_space_constraint(lax.all_to_all(buf, "dom", 0, 0), pltpu.HBM)
    outer, reg_part = call(
        inner_second_kernel, (state, reg, geometry, g, grad, link), (wave, state_shape), [], "inner_again", 20_000_000
    )
    sol, reg, absorbed = call(
        functools.partial(last_kernel, NMAT / (devices * elems)),
        (state, normals, link, orient, half_scale, refl, g, outer, recv, reg_part, lift_high, lift_low),
        (swapped, swapped, shape((2, NMAT), F32)),
        [flux_scratch, lift_scratch, state_scratch, state_scratch, blocks, all_losses, sems],
        "last",
        skip=(8,),
    )
    return sol.transpose(1, 0, 2), reg.transpose(1, 0, 2), absorbed


def solution(mesh):
    in_specs = (
        P(None, None, "dom"),
        P(None, None, "dom"),
        P(None, "dom"),
        P(None, None, "dom"),
        P(None, "dom"),
        P(),
        P(None, "dom"),
        P(None, "dom"),
        P(None, "dom"),
        P("dom", None),
    )
    out_specs = (P(None, None, "dom"), P(None, None, "dom"), P())
    return jax.shard_map(local, mesh=mesh, in_specs=in_specs, out_specs=out_specs, check_vma=False)
```

time: 75.2 us -> 64.9 us (0.86)
  local copies, waits for them, and re-layouts: 9.12 us -> 1.71 us
  Pallas kernels: 38 us -> 35.5 us
  waiting for transfers between devices: 10.2 us -> 8.56 us
  starting transfers between devices: 16.8 us -> 18.1 us
    pallas_call x2 -> x0, local copies, waits for them, and re-layouts: 3.73 us -> none  [call(): pl.pallas_call(body, out_shape=outs, in_specs=specs, out_specs=jax.tree.m...]
    unnamed x10 -> x4, local copies, waits for them, and re-layouts: 5.39 us -> 1.71 us
    pallas_call x5, Pallas kernels: 38 us -> 35.5 us  [call(): pl.pallas_call(kernel, out_shape=outs, in_specs=[SMEM if a.ndim == 1 else...]
    all_to_all x2, waiting for transfers between devices: 10.2 us -> 8.56 us  [local(): lax.all_to_all(buf, 'dom', 0, 0)]
    all_to_all x2, starting transfers between devices: 16.8 us -> 18.1 us  [local(): lax.all_to_all(buf, 'dom', 0, 0)]
  transfers between devices with their start and end apart: 2 -> 2, of which waited for: 2 -> 2; matrix products, arithmetic and copies ran while one was open for 2% -> 0% of each run, Pallas kernels for 27% -> 34%
where the time goes in v2:
time: 64.9 us; the launch traced here: 64.5 us
  Pallas kernels  35.5 us (55%)
  starting transfers between devices  18.1 us (28%)
  waiting for transfers between devices  8.56 us (13%)
  local copies, waits for them, and re-layouts  1.71 us (3%)
  between operations  0.68 us (1%)
    pallas_call x5, Pallas kernels, call(): pl.pallas_call(kernel, out_shape=outs, in_specs=[SMEM if a.ndim == 1 else...  35.5 us
    all_to_all x2, starting transfers between devices, local(): lax.all_to_all(buf, 'dom', 0, 0)  18.1 us
    all_to_all x2, waiting for transfers between devices, local(): lax.all_to_all(buf, 'dom', 0, 0)  8.56 us
    unnamed x4, local copies, waits for them, and re-layouts  1.71 us
  transfers between devices with their start and end apart: 2, of which 2 were waited for; matrix products, arithmetic and copies ran while one was open for 0% of the time, Pallas kernels for 34%

profile of v2, /device:TPU:1, one launch (start us, length us, event | category | flops | bytes accessed | tf_op | source)
XLA Modules:
  0.0 64.5 jit_solution(3204478459221098362)
XLA Ops:
  0.6 3.3 %first.1 = (f32[1536,128]{1,0:T(8,128)}, f32[10,64,128]{2,1,0:T(8,128)}, f32[128,1,1280]{2,1,0:T(1,128)}) custom-call(f32[20,4,2048]{2,1,0:T(4,128)} %bitcast.4, f32[3,4,2048]{2,1,0:T(4,128)} %refs_1_.5, s32[8,128]{1,0:T(8,128)} %refs_7_.3), custom_call_target="tpu_custom_call" | custom-call | flops 2000000 | bytes 4000000 | tf_op jit(solution)/shard_map/first/pallas_call | solution.py:547
  3.9 11.5 %all-to-all-start = ((f32[128,1,1280]{2,1,0:T(1,128)}), f32[128,1,1280]{2,1,0:T(1,128)S(1)}, u32[]{:S(2)}, u32[]{:S(2)}) async-start(f32[128,1,1280]{2,1,0:T(1,128)} %get-tuple-element.31), calls=%async_computation | async-start | bytes 1310720 | tf_op jit(solution)/shard_map/all_to_all | solution.py:565
  15.5 11.8 %inner.1 = (f32[10,64,128]{2,1,0:T(8,128)}, f32[1536,128]{1,0:T(8,128)}, s32[64,128]{1,0:T(8,128)}, s32[64,128]{1,0:T(8,128)}, f32[64,128]{1,0:T(8,128)}, /*inde...) custom-call(f32[1536,128]{1,0:T(8,128)} %get-tuple-element.23.refs_0_, f32[20,4,2048]{2,1,0:T(4,128)} %bitcast.5, ...), custom_call_target="tpu_custom_call" | custom-call | flops 20000000 | bytes 4000000 | tf_op jit(solution)/shard_map/inner/pallas_call | solution.py:547
  27.3 3.2 %all-to-all-done.refs_10_ = f32[128,1,1280]{2,1,0:T(1,128)S(1)} async-done(((f32[128,1,1280]{2,1,0:T(1,128)}), f32[128,1,1280]{2,1,0:T(1,128)S(1)}, u32[]{:S(2)}, u32[]{:S(2)}) %all-to-all-start) | async-done | bytes 655392 | tf_op jit(solution)/shard_map/all_to_all | solution.py:565
  30.5 0.0 copy-start.1
  30.5 0.8 %copy-done.1 = f32[128,1,1280]{2,1,0:T(1,128)} copy-done((f32[128,1,1280]{2,1,0:T(1,128)}, f32[128,1,1280]{2,1,0:T(1,128)S(1)}, u32[]{:S(2)}) %copy-start.1) | copy-done | bytes 655384
  31.3 5.0 %middle.1 = (f32[1536,128]{1,0:T(8,128)}, f32[1536,128]{1,0:T(8,128)}, f32[10,64,128]{2,1,0:T(8,128)}, f32[128,1,1408]{2,1,0:T(1,128)}) custom-call(f32[1536,128]{1,0:T(8,128)} %get-tuple-element.23.refs_0_, f32[3,4,2048]{2,1,0:T(4,128)} %refs_1_.5, s32[64,128]{1,0:T(8,128)} %get-tuple-element.25.refs_2_.refs_5_, s32[64,128]{1,0:T(8,128)} %get-tuple-element.26.refs_3_, ...), custom_call_target="tpu_custom_call" | custom-call | flops 2000000 | bytes 4000000 | tf_op jit(solution)/shard_map/middle/pallas_call | solution.py:547
  36.3 6.6 %all-to-all-start.1 = ((f32[128,1,1408]{2,1,0:T(1,128)}), f32[128,1,1408]{2,1,0:T(1,128)S(1)}, u32[]{:S(2)}, u32[]{:S(2)}) async-start(f32[128,1,1408]{2,1,0:T(1,128)} %get-tuple-element.38), calls=%async_computation.1 | async-start | bytes 1441792 | tf_op jit(solution)/shard_map/all_to_all | solution.py:582
  43.0 10.3 %inner_again.1 = (f32[10,64,128]{2,1,0:T(8,128)}, f32[1536,128]{1,0:T(8,128)}) custom-call(f32[1536,128]{1,0:T(8,128)} %get-tuple-element.34.refs_0_, f32[1536,128]{1,0:T(8,128)} %get-tuple-element.36.refs_1_, f32[9,2048]{1,0:T(8,128)} %refs_2_.5, f32[10,64,128]{2,1,0:T(8,128)} %get-tuple-element.35.refs_3_.refs_6_, ...), custom_call_target="tpu_custom_call" | custom-call | flops 20000000 | bytes 4000000 | tf_op jit(solution)/shard_map/inner_again/pallas_call | solution.py:547
  53.3 5.4 %all-to-all-done.1.refs_8_ = f32[128,1,1408]{2,1,0:T(1,128)S(1)} async-done(((f32[128,1,1408]{2,1,0:T(1,128)}), f32[128,1,1408]{2,1,0:T(1,128)S(1)}, u32[]{:S(2)}, u32[]{:S(2)}) %all-to-all-start.1) | async-done | bytes 720928 | tf_op jit(solution)/shard_map/all_to_all | solution.py:582
  58.7 0.0 copy-start
  58.7 0.9 %copy-done = f32[128,1,1408]{2,1,0:T(1,128)} copy-done((f32[128,1,1408]{2,1,0:T(1,128)}, f32[128,1,1408]{2,1,0:T(1,128)S(1)}, u32[]{:S(2)}) %copy-start) | copy-done | bytes 720920
  59.6 5.0 %last.1 = (f32[20,4,2048]{2,1,0:T(4,128)}, f32[20,4,2048]{2,1,0:T(4,128)}, f32[2,16]{1,0:T(2,128)}) custom-call(f32[1536,128]{1,0:T(8,128)} %get-tuple-element.34.refs_0_, f32[3,4,2048]{2,1,0:T(4,128)} %refs_1_.5, s32[64,128]{1,0:T(8,128)} %get-tuple-element.25.refs_2_.refs_5_, s32[64,128]{1,0:T(8,128)} %get-tuple-element.26.refs_3_, ...), custom_call_target="tpu_custom_call" | custom-call | flops 2000000 | bytes 4000000 | tf_op jit(solution)/shard_map/last/pallas_call | solution.py:547
Async XLA Ops:
  3.9 26.5 %all-to-all-start = ((f32[128,1,1280]{2,1,0:T(1,128)}), f32[128,1,1280]{2,1,0:T(1,128)S(1)}, u32[]{:S(2)}, u32[]{:S(2)}) async-start(f32[128,1,1280]{2,1,0:T(1,128)} %get-tuple-element.31), calls=%async_computation | async-start | bytes 1310720 | tf_op jit(solution)/shard_map/all_to_all | solution.py:565
  30.5 0.8 %copy-start.1 = (f32[128,1,1280]{2,1,0:T(1,128)}, f32[128,1,1280]{2,1,0:T(1,128)S(1)}, u32[]{:S(2)}) copy-start(f32[128,1,1280]{2,1,0:T(1,128)S(1)} %all-to-all-done.refs_10_) | copy-start | bytes 1966084
  36.3 22.4 %all-to-all-start.1 = ((f32[128,1,1408]{2,1,0:T(1,128)}), f32[128,1,1408]{2,1,0:T(1,128)S(1)}, u32[]{:S(2)}, u32[]{:S(2)}) async-start(f32[128,1,1408]{2,1,0:T(1,128)} %get-tuple-element.38), calls=%async_computation.1 | async-start | bytes 1441792 | tf_op jit(solution)/shard_map/all_to_all | solution.py:582
  58.7 0.9 %copy-start = (f32[128,1,1408]{2,1,0:T(1,128)}, f32[128,1,1408]{2,1,0:T(1,128)S(1)}, u32[]{:S(2)}) copy-start(f32[128,1,1408]{2,1,0:T(1,128)S(1)} %all-to-all-done.1.refs_8_) | copy-start | bytes 2162692

commit v3 on v2

--- a/solution.py
+++ b/solution.py
@@ -135,6 +135,7 @@
 GRAD_ROWS, LIFT_ROWS, FACE_NODES, ROTATIONS = dg_tables()
 LIFT_CHUNKS = 4
 GRANT = None
+GRANTED = ('middle', 'last')
 BYTES = 4_000_000
 TILES = [(0, 8), (8, 8), (16, 4)]
 
@@ -182,9 +183,7 @@
             held[k] = refs[total + at]
         rest = refs[total + len(kept) : -1]
         stage = Staged(outside, held, refs[-1], count_in)
-        for k in kept:
-            if k < count_in:
-                stage.copy(k).start()
+        order = sorted((k for k in kept if k < count_in), key=lambda k: math.prod(held[k].shape))
         waited, sent = set(), set()
 
         def wait(*names):
@@ -198,6 +197,11 @@
                 sent.add(count_in + k)
                 stage.copy(count_in + k).start()
 
+        def begin():
+            for k in order:
+                stage.copy(k).start()
+
+        wait.begin = begin
         body(wait, emit, *held, *rest)
         wait(*[k for k in kept if k < count_in])
         emit(*[k - count_in for k in kept if k >= count_in and k not in sent])
@@ -219,22 +223,19 @@
             dst[row : row + 8, :] = convert(got)
 
 
-def spread(src, dst, chunks):
+def spread(src, dst, chunks, start=0, stop=None):
     def chunk(c, carry):
         for node in range(NODES):
             dst[pl.ds(c * 24 + node, 4, stride=chunks * 24), :] = src[node, :, lanes_of(c)]
         return carry
 
-    lax.fori_loop(0, chunks, chunk, 0, unroll=2)
-
-
-def collect(src, dst, chunks):
-    def chunk(c, carry):
+    lax.fori_loop(start, chunks if stop is None else stop, chunk, 0, unroll=4)
+
+
+def collect(src, dst, chunks, start, stop):
+    for c in range(start, stop):
         for node in range(NODES):
-            dst[node, :, lanes_of(c)] = src[pl.ds(c * 24 + node, 4, stride=chunks * 24), :]
-        return carry
-
-    lax.fori_loop(0, chunks, chunk, 0, unroll=2)
+            dst[node, :, c * LANES : (c + 1) * LANES] = src[pl.ds(c * 24 + node, 4, stride=chunks * 24), :]
 
 
 def state_rows(field, c, chunks, start, size):
@@ -322,25 +323,33 @@
     return totals
 
 
-def first_kernel(wait, emit, sol, normals, send_faces, state, g, buf, waves, outgoing, sems):
+def first_kernel(wait, emit, sol_in, normals, send_faces, state, g, buf, waves, sol, outgoing, sems):
     chunks = sol.shape[2] // LANES
-    wait(0)
-    spread(sol, state, chunks)
-    emit(0)
-    wait(1)
+    part = chunks // 4
+    copies = []
+    for q in range(4):
+        at = pl.ds(q * part * LANES, part * LANES)
+        copies.append(pltpu.make_async_copy(sol_in.at[:, :, at], sol.at[:, :, at], sems.at[q]))
+        copies[-1].start()
+    wait.begin()
 
     def chunk(c, carry):
         fields = [[state[state_rows(i, c, chunks, start, size), :] for start, size in TILES] for i in range(4)]
         wave_tiles(fields, c, chunks, normals, waves)
         return carry
 
-    lax.fori_loop(0, chunks, chunk, 0, unroll=2)
+    wait(1)
+    for q in range(4):
+        copies[q].wait()
+        spread(sol, state, chunks, q * part, (q + 1) * part)
+        lax.fori_loop(q * part, (q + 1) * part, chunk, 0, unroll=2)
+    emit(0)
     wait(2)
     pack(chunks, waves, send_faces, g, outgoing, lambda: emit(1))
     post(outgoing, buf, sems)()
 
 
-def inside(decay, chunks, state, reg, geometry, link, g, grad, out_g, out_reg):
+def inside(decay, chunks, state, reg, geometry, link, refl, half_scale, g, grad, out_g, out_reg, out_base, prepare, finished):
     def volume(b, carry):
         def pair(ref, field):
             return jnp.concatenate([ref[state_rows(field, 2 * b + k, chunks, 0, NODES), :] for k in (0, 1)], axis=1)
@@ -366,8 +375,6 @@
                 out_reg[rows, :] = decay * reg[rows, :] - time_step * results[i][:, k * LANES : (k + 1) * LANES]
         return carry
 
-    lax.fori_loop(0, chunks // 2, volume, 0)
-
     def group(j, carry):
         codes = link[rows_of(j), :]
         low = codes & (LANES - 1)
@@ -381,33 +388,57 @@
             out_g[n, rows_of(j), :] = acc[n]
         return carry
 
-    lax.fori_loop(0, 4 * chunks // 8, group, 0)
-
-
-def inner_first_kernel(wait, emit, state, reg, geometry, g, grad, neighbour, orientation, material, scale, impedance, out_g, out_reg, link, orient, half_scale, refl, mat, totals, reg_rows, tmp, tmp_int):
+    lax.fori_loop(0, chunks // 4, group, 0)
+    prepare()
+    for f in range(4):
+        for part in range(chunks // 8):
+            row = f * chunks + part * 8
+            rows = slice(row, row + 8)
+            mirror = jnp.where(link[rows, :] < 0, 1.0 + refl[rows, :], 1.0)
+            for n in range(10):
+                press = at_face(state, 0, chunks, part, FACE_NODES[f][n])
+                out_base[n, rows, :] = half_scale[rows, :] * (mirror * g[n, rows, :] - 2.0 * press)
+    lax.fori_loop(0, chunks // 2, volume, 0)
+    finished()
+    lax.fori_loop(chunks // 4, chunks // 2, group, 0)
+
+
+def inner_first_kernel(wait, emit, state, reg, geometry, g, grad, neighbour, orientation, material, scale, impedance, out_g, out_reg, out_base, link, orient, half_scale, refl, mat, totals, reg_rows, tmp, tmp_int):
     chunks = neighbour.shape[1] // LANES
-    wait(*range(9))
+    wait.begin()
+    wait(5, 3)
     faces_to_rows(neighbour, tmp_int, link, lambda x: x)
-    faces_to_rows(orientation, tmp_int, orient, lambda x: x)
-    faces_to_rows(scale, tmp, half_scale, lambda x: 0.5 * x)
-    faces_to_rows(material, tmp_int, mat, lambda x: x)
-    for row in range(0, 4 * chunks, 8):
-        key = mat[row : row + 8, :]
-        picked = jnp.zeros((8, LANES), F32)
-        for m in range(NMAT):
-            picked = jnp.where(key == m, impedance[m], picked)
-        refl[row : row + 8, :] = (picked - 1.0) / (picked + 1.0)
-    totals[...] = wall_losses(0, chunks, g, link, refl, half_scale, mat, jnp.zeros((1, LANES), F32))
-    spread(reg, reg_rows, chunks)
-    inside(section_decay[0], chunks, state, reg_rows, geometry, link, g, grad, out_g, out_reg)
-
-
-def inner_second_kernel(wait, emit, state, reg, geometry, g, grad, link, out_g, out_reg):
-    wait(*range(6))
-    inside(section_decay[1], geometry.shape[1] // LANES, state, reg, geometry, link, g, grad, out_g, out_reg)
-
-
-def finish(section, chunks, state, normals, link, orient, half_scale, refl, g, outer, incoming, reg_part, lift_high, lift_low, new_state, new_reg, flux_acc, lift_acc, ready, after):
+    emit(3)
+
+    def prepare():
+        wait(6, 7, 8)
+        faces_to_rows(orientation, tmp_int, orient, lambda x: x)
+        faces_to_rows(scale, tmp, half_scale, lambda x: 0.5 * x)
+        faces_to_rows(material, tmp_int, mat, lambda x: x)
+        emit(4, 5, 7)
+        for row in range(0, 4 * chunks, 8):
+            key = mat[row : row + 8, :]
+            picked = jnp.zeros((8, LANES), F32)
+            for m in range(NMAT):
+                picked = jnp.where(key == m, impedance[m], picked)
+            refl[row : row + 8, :] = (picked - 1.0) / (picked + 1.0)
+        emit(6)
+        totals[...] = wall_losses(0, chunks, g, link, refl, half_scale, mat, jnp.zeros((1, LANES), F32))
+        emit(8)
+        wait(1)
+        spread(reg, reg_rows, chunks)
+        wait(0, 2, 4)
+
+    inside(section_decay[0], chunks, state, reg_rows, geometry, link, refl, half_scale, g, grad, out_g, out_reg, out_base, prepare, lambda: emit(1, 2))
+
+
+def inner_second_kernel(wait, emit, state, reg, geometry, g, grad, link, refl, half_scale, out_g, out_reg, out_base):
+    wait.begin()
+    wait(3, 5)
+    inside(section_decay[1], geometry.shape[1] // LANES, state, reg, geometry, link, refl, half_scale, g, grad, out_g, out_reg, out_base, lambda: wait(0, 1, 2, 4, 6, 7), lambda: emit(1, 2))
+
+
+def finish(section, chunks, state, normals, link, orient, half_scale, base, outer, incoming, reg_part, lift_high, lift_low, new_state, new_reg, flux_acc, lift_acc, ready, after, quarter=None):
     local_faces = 4 * chunks
     for f in range(4):
         for part in range(chunks // 8):
@@ -424,16 +455,12 @@
                     acc[n] = jnp.where(here, lookup(got, low), acc[n])
             turn = orient[rows, :]
             wall = codes < 0
-            r = refl[rows, :]
             scale = half_scale[rows, :]
             for n in range(10):
                 a, b, c = (ROTATIONS[t][n] for t in range(3))
                 turned = acc[a] if a == b == c else jnp.where(turn == 0, acc[a], jnp.where(turn == 1, acc[b], acc[c]))
-                own = g[n, rows, :]
-                turned = own + jnp.where(wall, r * own, turned)
-                press = at_face(state, 0, chunks, part, FACE_NODES[f][n])
                 k = f * 10 + n
-                flux_acc[k // 8, pl.ds(part * 64 + k % 8, 8, stride=8), :] = scale * (turned - 2.0 * press)
+                flux_acc[k // 8, pl.ds(part * 64 + k % 8, 8, stride=8), :] = base[n, rows, :] + jnp.where(wall, 0.0, scale * turned)
 
     for c in range(0, chunks, LIFT_CHUNKS):
         flux = split_bf16(
@@ -469,47 +496,67 @@
         after(c, fields)
         return carry
 
-    lax.fori_loop(0, chunks, chunk, 0, unroll=4)
-
-
-def middle_kernel(wait, emit, state, normals, link, orient, half_scale, refl, mat, send_faces, g, outer, recv, reg_part, lift_high, lift_low, totals_in, new_state, new_reg, new_g, buf, flux_acc, lift_acc, waves, outgoing, incoming, losses, sems):
+    if quarter is None:
+        lax.fori_loop(0, chunks, chunk, 0, unroll=4)
+    else:
+        for q in range(4):
+            lax.fori_loop(q * chunks // 4, (q + 1) * chunks // 4, chunk, 0, unroll=True)
+            quarter(q)
+
+
+def middle_kernel(wait, emit, state, normals, link, orient, half_scale, refl, mat, send_faces, base, outer, recv, reg_part, lift_high, lift_low, totals_in, new_state, new_reg, new_g, buf, flux_acc, lift_acc, waves, outgoing, incoming, losses, sems):
     chunks = normals.shape[2] // LANES
     arrived = collect_blocks(recv, incoming, sems)
-    wait(0, 2, 3, 4, 5, 8, 9, 12, 13)
+    wait.begin()
+    wait(2, 3, 4, 8, 9, 12, 13)
     arrived()
 
     def after(c, fields):
         wave_tiles(fields, c, chunks, normals, waves)
 
-    finish(0, chunks, state, normals, link, orient, half_scale, refl, g, outer, incoming, reg_part, lift_high, lift_low, new_state, new_reg, flux_acc, lift_acc, lambda: wait(1, 11), after)
+    finish(0, chunks, state, normals, link, orient, half_scale, base, outer, incoming, reg_part, lift_high, lift_low, new_state, new_reg, flux_acc, lift_acc, lambda: wait(0, 1, 11), after)
     emit(0, 1)
-    wait(6, 7, 14)
-    pack(chunks, waves, send_faces, new_g, outgoing, lambda: emit(2))
+    wait(5, 6, 7, 14)
+    copy = pltpu.make_async_copy(losses, buf.at[:, 0, pl.ds(10 * LANES, LANES)], sems.at[8])
+
+    def filled():
+        emit(2)
+        totals = wall_losses(1, chunks, new_g, link, refl, half_scale, mat, totals_in[...])
+        losses[...] = jnp.broadcast_to(totals, losses.shape)
+        copy.start()
+
+    pack(chunks, waves, send_faces, new_g, outgoing, filled)
     posted = post(outgoing, buf, sems)
-    totals = wall_losses(1, chunks, new_g, link, refl, half_scale, mat, totals_in[...])
-    losses[...] = jnp.broadcast_to(totals, losses.shape)
-    copy = pltpu.make_async_copy(losses, buf.at[:, 0, pl.ds(10 * LANES, LANES)], sems.at[8])
-    copy.start()
     posted()
     copy.wait()
 
 
-def last_kernel(norm_factor, wait, emit, state, normals, link, orient, half_scale, refl, g, outer, recv, reg_part, lift_high, lift_low, new_sol, new_reg, absorbed, flux_acc, lift_acc, sol_rows, reg_rows, incoming, losses, sems):
+def last_kernel(norm_factor, wait, emit, state, normals, link, orient, half_scale, base, outer, recv, reg_part, lift_high, lift_low, out_sol, out_reg, absorbed, flux_acc, lift_acc, sol_rows, reg_rows, new_sol, new_reg, incoming, losses, sems):
     chunks = normals.shape[2] // LANES
     arrived = collect_blocks(recv, incoming, sems)
     copy = pltpu.make_async_copy(recv.at[:, 0, pl.ds(10 * LANES, LANES)], losses, sems.at[8])
     copy.start()
-    wait(0, 2, 3, 4, 5, 6, 7, 10, 11)
+    wait.begin()
+    wait(2, 3, 4, 5, 6, 9, 10)
     arrived()
-    finish(1, chunks, state, normals, link, orient, half_scale, refl, g, outer, incoming, reg_part, lift_high, lift_low, sol_rows, reg_rows, flux_acc, lift_acc, lambda: wait(1, 9), lambda c, fields: None)
-    collect(reg_rows, new_reg, chunks)
-    emit(1)
-    collect(sol_rows, new_sol, chunks)
-    emit(0)
+    copies = []
+
+    def quarter(q):
+        part = chunks // 4
+        at = pl.ds(q * part * LANES, part * LANES)
+        for k, (src, held, dst) in enumerate(((sol_rows, new_sol, out_sol), (reg_rows, new_reg, out_reg))):
+            collect(src, held, chunks, q * part, (q + 1) * part)
+            copies.append(pltpu.make_async_copy(held.at[:, :, at], dst.at[:, :, at], sems.at[9 + 2 * q + k]))
+            copies[-1].start()
+
+    finish(1, chunks, state, normals, link, orient, half_scale, base, outer, incoming, reg_part, lift_high, lift_low, sol_rows, reg_rows, flux_acc, lift_acc, lambda: wait(0, 1, 8), lambda c, fields: None, quarter)
     copy.wait()
     total = jnp.sum(losses[...], axis=0, keepdims=True) * norm_factor
     absorbed[0:1, :] = total[:, 0:NMAT]
     absorbed[1:2, :] = total[:, NMAT : 2 * NMAT]
+    emit(2)
+    for each in copies:
+        each.wait()
 
 
 def local(solution, register, geometry, normals, face_scale, impedance, neighbour, orientation, wall_material, send_faces):
@@ -552,7 +599,7 @@
             scratch_shapes=[pltpu.VMEM(arrays[k].shape, arrays[k].dtype) for k in kept]
             + scratch
             + [pltpu.SemaphoreType.DMA((total,))],
-            compiler_params=pltpu.CompilerParams(vmem_limit_bytes=GRANT),
+            compiler_params=pltpu.CompilerParams(vmem_limit_bytes=GRANT if name in GRANTED else None),
             cost_estimate=pl.CostEstimate(flops=flops, bytes_accessed=BYTES, transcendentals=0),
             name=name,
         )(*args)
@@ -561,35 +608,37 @@
     all_losses = pltpu.VMEM((devices, LANES), F32)
     sems = pltpu.SemaphoreType.DMA((9,))
     turned = solution.transpose(1, 0, 2)
-    state, g, buf = call(first_kernel, (turned, normals, send_faces), (state_shape, wave, packet(10)), [state_scratch, blocks, sems], "first", skip=(5,))
-    recv = pltpu.with_memory_space_constraint(lax.all_to_all(buf, "dom", 0, 0), pltpu.HBM)
-    outer, reg_part, link, orient, half_scale, refl, mat, totals = call(
+    state, g, buf = call(first_kernel, (turned, normals, send_faces), (state_shape, wave, packet(10)), [state_scratch, pltpu.VMEM(swapped.shape, F32), blocks, sems], "first", skip=(0, 5))
+    recv = lax.all_to_all(buf, "dom", 0, 0)
+    outer, reg_part, base, link, orient, half_scale, refl, mat, totals = call(
         inner_first_kernel,
         (state, register.transpose(1, 0, 2), geometry, g, grad, neighbour, orientation, wall_material, face_scale, impedance),
-        (wave, state_shape, plane_int, plane_int, plane, plane, plane_int, line),
+        (wave, state_shape, wave, plane_int, plane_int, plane, plane, plane_int, line),
         [state_scratch, pltpu.VMEM((8 * chunks, LANES), F32), pltpu.VMEM((8 * chunks, LANES), jnp.int32)],
         "inner",
         20_000_000,
     )
     state, reg, g, buf = call(
         middle_kernel,
-        (state, normals, link, orient, half_scale, refl, mat, send_faces, g, outer, recv, reg_part, lift_high, lift_low, totals),
+        (state, normals, link, orient, half_scale, refl, mat, send_faces, base, outer, recv, reg_part, lift_high, lift_low, totals),
         (state_shape, state_shape, wave, packet(11)),
         [flux_scratch, lift_scratch, state_scratch, blocks, blocks, all_losses, sems],
         "middle",
         skip=(10, 18),
     )
-    recv = pltpu.with_memory_space_constraint(lax.all_to_all(buf, "dom", 0, 0), pltpu.HBM)
-    outer, reg_part = call(
-        inner_second_kernel, (state, reg, geometry, g, grad, link), (wave, state_shape), [], "inner_again", 20_000_000
+    recv = lax.all_to_all(buf, "dom", 0, 0)
+    outer, reg_part, base = call(
+        inner_second_kernel, (state, reg, geometry, g, grad, link, refl, half_scale), (wave, state_shape, wave), [], "inner_again", 20_000_000
     )
     sol, reg, absorbed = call(
         functools.partial(last_kernel, NMAT / (devices * elems)),
-        (state, normals, link, orient, half_scale, refl, g, outer, recv, reg_part, lift_high, lift_low),
+        (state, normals, link, orient, half_scale, base, outer, recv, reg_part, lift_high, lift_low),
         (swapped, swapped, shape((2, NMAT), F32)),
-        [flux_scratch, lift_scratch, state_scratch, state_scratch, blocks, all_losses, sems],
+        [flux_scratch, lift_scratch, state_scratch, state_scratch]
+        + [pltpu.VMEM(swapped.shape, F32)] * 2
+        + [blocks, all_losses, pltpu.SemaphoreType.DMA((17,))],
         "last",
-        skip=(8,),
+        skip=(7, 11, 12),
     )
     return sol.transpose(1, 0, 2), reg.transpose(1, 0, 2), absorbed
 

time: 64.9 us -> 63.7 us (0.982)
  Pallas kernels: 35.5 us -> 33.7 us
  waiting for transfers between devices: 8.56 us -> 9.7 us
    pallas_call x5, Pallas kernels: 35.5 us -> 33.7 us  [call(): pl.pallas_call(kernel, out_shape=outs, in_specs=[SMEM if a.ndim == 1 else...]
    all_to_all x2, waiting for transfers between devices: 8.56 us -> 9.7 us  [local(): recv = lax.all_to_all(buf, 'dom', 0, 0)]
  transfers between devices with their start and end apart: 2 -> 2, of which waited for: 2 -> 2; matrix products, arithmetic and copies ran while one was open for 0% -> 0% of each run, Pallas kernels for 34% -> 33%
where the time goes in v3:
time: 63.7 us; the launch traced here: 63.3 us
  Pallas kernels  33.7 us (53%)
  starting transfers between devices  17.5 us (27%)
  waiting for transfers between devices  9.7 us (15%)
  local copies, waits for them, and re-layouts  1.71 us (3%)
  between operations  0.68 us (1%)
    pallas_call x5, Pallas kernels, call(): pl.pallas_call(kernel, out_shape=outs, in_specs=[SMEM if a.ndim == 1 else...  33.7 us
    all_to_all x2, starting transfers between devices, local(): recv = lax.all_to_all(buf, 'dom', 0, 0)  17.5 us
    all_to_all x2, waiting for transfers between devices, local(): recv = lax.all_to_all(buf, 'dom', 0, 0)  9.7 us
    unnamed x4, local copies, waits for them, and re-layouts  1.71 us
  transfers between devices with their start and end apart: 2, of which 2 were waited for; matrix products, arithmetic and copies ran while one was open for 0% of the time, Pallas kernels for 33%

profile of v3, /device:TPU:1, one launch (start us, length us, event | category | flops | bytes accessed | tf_op | source)
XLA Modules:
  0.0 63.3 jit_solution(15469843423471279291)
XLA Ops:
  0.6 3.4 %first.1 = (f32[1536,128]{1,0:T(8,128)}, f32[10,64,128]{2,1,0:T(8,128)}, f32[128,1,1280]{2,1,0:T(1,128)}) custom-call(f32[20,4,2048]{2,1,0:T(4,128)} %bitcast.4, f32[3,4,2048]{2,1,0:T(4,128)} %refs_1_.5, s32[8,128]{1,0:T(8,128)} %refs_7_.3), custom_call_target="tpu_custom_call" | custom-call | flops 2000000 | bytes 4000000 | tf_op jit(solution)/shard_map/first/pallas_call | solution.py:594
  4.0 11.5 %all-to-all-start = ((f32[128,1,1280]{2,1,0:T(1,128)}), f32[128,1,1280]{2,1,0:T(1,128)S(1)}, u32[]{:S(2)}, u32[]{:S(2)}) async-start(f32[128,1,1280]{2,1,0:T(1,128)} %get-tuple-element.34), calls=%async_computation | async-start | bytes 1310720 | tf_op jit(solution)/shard_map/all_to_all | solution.py:612
  15.6 11.3 %inner.1 = (f32[10,64,128]{2,1,0:T(8,128)}, f32[1536,128]{1,0:T(8,128)}, f32[10,64,128]{2,1,0:T(8,128)}, s32[64,128]{1,0:T(8,128)}, s32[64,128]{1,0:T(8,128)}, /...) custom-call(f32[1536,128]{1,0:T(8,128)} %get-tuple-element.25.refs_0_, ...), custom_call_target="tpu_custom_call" | custom-call | flops 20000000 | bytes 4000000 | tf_op jit(solution)/shard_map/inner/pallas_call | solution.py:594
  26.8 3.7 %all-to-all-done.refs_10_ = f32[128,1,1280]{2,1,0:T(1,128)S(1)} async-done(((f32[128,1,1280]{2,1,0:T(1,128)}), f32[128,1,1280]{2,1,0:T(1,128)S(1)}, u32[]{:S(2)}, u32[]{:S(2)}) %all-to-all-start) | async-done | bytes 655392 | tf_op jit(solution)/shard_map/all_to_all | solution.py:612
  30.6 0.0 copy-start.1
  30.6 0.8 %copy-done.1 = f32[128,1,1280]{2,1,0:T(1,128)} copy-done((f32[128,1,1280]{2,1,0:T(1,128)}, f32[128,1,1280]{2,1,0:T(1,128)S(1)}, u32[]{:S(2)}) %copy-start.1) | copy-done | bytes 655384
  31.4 4.8 %middle.1 = (f32[1536,128]{1,0:T(8,128)}, f32[1536,128]{1,0:T(8,128)}, f32[10,64,128]{2,1,0:T(8,128)}, f32[128,1,1408]{2,1,0:T(1,128)}) custom-call(f32[1536,128]{1,0:T(8,128)} %get-tuple-element.25.refs_0_, f32[3,4,2048]{2,1,0:T(4,128)} %refs_1_.5, s32[64,128]{1,0:T(8,128)} %get-tuple-element.27.refs_2_.refs_5_, s32[64,128]{1,0:T(8,128)} %get-tuple-element.28.refs_3_, ...), custom_call_target="tpu_custom_call" | custom-call | flops 2000000 | bytes 4000000 | tf_op jit(solution)/shard_map/middle/pallas_call | solution.py:594
  36.2 6.0 %all-to-all-start.1 = ((f32[128,1,1408]{2,1,0:T(1,128)}), f32[128,1,1408]{2,1,0:T(1,128)S(1)}, u32[]{:S(2)}, u32[]{:S(2)}) async-start(f32[128,1,1408]{2,1,0:T(1,128)} %get-tuple-element.42), calls=%async_computation.1 | async-start | bytes 1441792 | tf_op jit(solution)/shard_map/all_to_all | solution.py:629
  42.3 9.8 %inner_again.1 = (f32[10,64,128]{2,1,0:T(8,128)}, f32[1536,128]{1,0:T(8,128)}, f32[10,64,128]{2,1,0:T(8,128)}) custom-call(f32[1536,128]{1,0:T(8,128)} %get-tuple-element.37.refs_0_, f32[1536,128]{1,0:T(8,128)} %get-tuple-element.38.refs_1_, f32[9,2048]{1,0:T(8,128)} %refs_2_.5, f32[10,64,128]{2,1,0:T(8,128)} %get-tuple-element.39.refs_3_, ...), custom_call_target="tpu_custom_call" | custom-call | flops 20000000 | bytes 4000000 | tf_op jit(solution)/shard_map/inner_again/pallas_call | solution.py:594
  52.0 6.0 %all-to-all-done.1.refs_7_ = f32[128,1,1408]{2,1,0:T(1,128)S(1)} async-done(((f32[128,1,1408]{2,1,0:T(1,128)}), f32[128,1,1408]{2,1,0:T(1,128)S(1)}, u32[]{:S(2)}, u32[]{:S(2)}) %all-to-all-start.1) | async-done | bytes 720928 | tf_op jit(solution)/shard_map/all_to_all | solution.py:629
  58.0 0.0 copy-start
  58.0 0.9 %copy-done = f32[128,1,1408]{2,1,0:T(1,128)} copy-done((f32[128,1,1408]{2,1,0:T(1,128)}, f32[128,1,1408]{2,1,0:T(1,128)S(1)}, u32[]{:S(2)}) %copy-start) | copy-done | bytes 720920
  58.8 4.5 %last.1 = (f32[20,4,2048]{2,1,0:T(4,128)}, f32[20,4,2048]{2,1,0:T(4,128)}, f32[2,16]{1,0:T(2,128)}) custom-call(f32[1536,128]{1,0:T(8,128)} %get-tuple-element.37.refs_0_, f32[3,4,2048]{2,1,0:T(4,128)} %refs_1_.5, s32[64,128]{1,0:T(8,128)} %get-tuple-element.27.refs_2_.refs_5_, s32[64,128]{1,0:T(8,128)} %get-tuple-element.28.refs_3_, ...), custom_call_target="tpu_custom_call" | custom-call | flops 2000000 | bytes 4000000 | tf_op jit(solution)/shard_map/last/pallas_call | solution.py:594
Async XLA Ops:
  4.0 26.5 %all-to-all-start = ((f32[128,1,1280]{2,1,0:T(1,128)}), f32[128,1,1280]{2,1,0:T(1,128)S(1)}, u32[]{:S(2)}, u32[]{:S(2)}) async-start(f32[128,1,1280]{2,1,0:T(1,128)} %get-tuple-element.34), calls=%async_computation | async-start | bytes 1310720 | tf_op jit(solution)/shard_map/all_to_all | solution.py:612
  30.6 0.8 %copy-start.1 = (f32[128,1,1280]{2,1,0:T(1,128)}, f32[128,1,1280]{2,1,0:T(1,128)S(1)}, u32[]{:S(2)}) copy-start(f32[128,1,1280]{2,1,0:T(1,128)S(1)} %all-to-all-done.refs_10_) | copy-start | bytes 1966084
  36.2 21.8 %all-to-all-start.1 = ((f32[128,1,1408]{2,1,0:T(1,128)}), f32[128,1,1408]{2,1,0:T(1,128)S(1)}, u32[]{:S(2)}, u32[]{:S(2)}) async-start(f32[128,1,1408]{2,1,0:T(1,128)} %get-tuple-element.42), calls=%async_computation.1 | async-start | bytes 1441792 | tf_op jit(solution)/shard_map/all_to_all | solution.py:629
  58.0 0.9 %copy-start = (f32[128,1,1408]{2,1,0:T(1,128)}, f32[128,1,1408]{2,1,0:T(1,128)S(1)}, u32[]{:S(2)}) copy-start(f32[128,1,1408]{2,1,0:T(1,128)S(1)} %all-to-all-done.1.refs_7_) | copy-start | bytes 2162692

commit v4 on v3

--- a/solution.py
+++ b/solution.py
@@ -135,6 +135,7 @@
 GRAD_ROWS, LIFT_ROWS, FACE_NODES, ROTATIONS = dg_tables()
 LIFT_CHUNKS = 4
 GRANT = None
+UNROLL = 8
 GRANTED = ('middle', 'last')
 BYTES = 4_000_000
 TILES = [(0, 8), (8, 8), (16, 4)]
@@ -497,7 +498,7 @@
         return carry
 
     if quarter is None:
-        lax.fori_loop(0, chunks, chunk, 0, unroll=4)
+        lax.fori_loop(0, chunks, chunk, 0, unroll=UNROLL)
     else:
         for q in range(4):
             lax.fori_loop(q * chunks // 4, (q + 1) * chunks // 4, chunk, 0, unroll=True)

time: 63.7 us -> 63.6 us (level)
  no operation moved by 1% of the time
where the time goes in v4:
time: 63.6 us; the launch traced here: 63.3 us
  Pallas kernels  33.7 us (53%)
  starting transfers between devices  17.5 us (28%)
  waiting for transfers between devices  9.7 us (15%)
  local copies, waits for them, and re-layouts  1.71 us (3%)
  between operations  0.68 us (1%)
    pallas_call x5, Pallas kernels, call(): pl.pallas_call(kernel, out_shape=outs, in_specs=[SMEM if a.ndim == 1 else...  33.7 us
    all_to_all x2, starting transfers between devices, local(): recv = lax.all_to_all(buf, 'dom', 0, 0)  17.5 us
    all_to_all x2, waiting for transfers between devices, local(): recv = lax.all_to_all(buf, 'dom', 0, 0)  9.7 us
    unnamed x4, local copies, waits for them, and re-layouts  1.71 us
  transfers between devices with their start and end apart: 2, of which 2 were waited for; matrix products, arithmetic and copies ran while one was open for 0% of the time, Pallas kernels for 33%

profile of v4, /device:TPU:1, one launch (start us, length us, event | category | flops | bytes accessed | tf_op | source)
XLA Modules:
  0.0 63.3 jit_solution(16546366776627613541)
XLA Ops:
  0.6 3.4 %first.1 = (f32[1536,128]{1,0:T(8,128)}, f32[10,64,128]{2,1,0:T(8,128)}, f32[128,1,1280]{2,1,0:T(1,128)}) custom-call(f32[20,4,2048]{2,1,0:T(4,128)} %bitcast.4, f32[3,4,2048]{2,1,0:T(4,128)} %refs_1_.5, s32[8,128]{1,0:T(8,128)} %refs_7_.3), custom_call_target="tpu_custom_call" | custom-call | flops 2000000 | bytes 4000000 | tf_op jit(solution)/shard_map/first/pallas_call | solution.py:595
  4.0 11.5 %all-to-all-start = ((f32[128,1,1280]{2,1,0:T(1,128)}), f32[128,1,1280]{2,1,0:T(1,128)S(1)}, u32[]{:S(2)}, u32[]{:S(2)}) async-start(f32[128,1,1280]{2,1,0:T(1,128)} %get-tuple-element.34), calls=%async_computation | async-start | bytes 1310720 | tf_op jit(solution)/shard_map/all_to_all | solution.py:613
  15.6 11.3 %inner.1 = (f32[10,64,128]{2,1,0:T(8,128)}, f32[1536,128]{1,0:T(8,128)}, f32[10,64,128]{2,1,0:T(8,128)}, s32[64,128]{1,0:T(8,128)}, s32[64,128]{1,0:T(8,128)}, /...) custom-call(f32[1536,128]{1,0:T(8,128)} %get-tuple-element.25.refs_0_, ...), custom_call_target="tpu_custom_call" | custom-call | flops 20000000 | bytes 4000000 | tf_op jit(solution)/shard_map/inner/pallas_call | solution.py:595
  26.8 3.7 %all-to-all-done.refs_10_ = f32[128,1,1280]{2,1,0:T(1,128)S(1)} async-done(((f32[128,1,1280]{2,1,0:T(1,128)}), f32[128,1,1280]{2,1,0:T(1,128)S(1)}, u32[]{:S(2)}, u32[]{:S(2)}) %all-to-all-start) | async-done | bytes 655392 | tf_op jit(solution)/shard_map/all_to_all | solution.py:613
  30.6 0.0 copy-start.1
  30.6 0.8 %copy-done.1 = f32[128,1,1280]{2,1,0:T(1,128)} copy-done((f32[128,1,1280]{2,1,0:T(1,128)}, f32[128,1,1280]{2,1,0:T(1,128)S(1)}, u32[]{:S(2)}) %copy-start.1) | copy-done | bytes 655384
  31.4 4.8 %middle.1 = (f32[1536,128]{1,0:T(8,128)}, f32[1536,128]{1,0:T(8,128)}, f32[10,64,128]{2,1,0:T(8,128)}, f32[128,1,1408]{2,1,0:T(1,128)}) custom-call(f32[1536,128]{1,0:T(8,128)} %get-tuple-element.25.refs_0_, f32[3,4,2048]{2,1,0:T(4,128)} %refs_1_.5, s32[64,128]{1,0:T(8,128)} %get-tuple-element.27.refs_2_.refs_5_, s32[64,128]{1,0:T(8,128)} %get-tuple-element.28.refs_3_, ...), custom_call_target="tpu_custom_call" | custom-call | flops 2000000 | bytes 4000000 | tf_op jit(solution)/shard_map/middle/pallas_call | solution.py:595
  36.2 6.0 %all-to-all-start.1 = ((f32[128,1,1408]{2,1,0:T(1,128)}), f32[128,1,1408]{2,1,0:T(1,128)S(1)}, u32[]{:S(2)}, u32[]{:S(2)}) async-start(f32[128,1,1408]{2,1,0:T(1,128)} %get-tuple-element.42), calls=%async_computation.1 | async-start | bytes 1441792 | tf_op jit(solution)/shard_map/all_to_all | solution.py:630
  42.2 9.8 %inner_again.1 = (f32[10,64,128]{2,1,0:T(8,128)}, f32[1536,128]{1,0:T(8,128)}, f32[10,64,128]{2,1,0:T(8,128)}) custom-call(f32[1536,128]{1,0:T(8,128)} %get-tuple-element.37.refs_0_, f32[1536,128]{1,0:T(8,128)} %get-tuple-element.38.refs_1_, f32[9,2048]{1,0:T(8,128)} %refs_2_.5, f32[10,64,128]{2,1,0:T(8,128)} %get-tuple-element.39.refs_3_, ...), custom_call_target="tpu_custom_call" | custom-call | flops 20000000 | bytes 4000000 | tf_op jit(solution)/shard_map/inner_again/pallas_call | solution.py:595
  52.0 6.0 %all-to-all-done.1.refs_7_ = f32[128,1,1408]{2,1,0:T(1,128)S(1)} async-done(((f32[128,1,1408]{2,1,0:T(1,128)}), f32[128,1,1408]{2,1,0:T(1,128)S(1)}, u32[]{:S(2)}, u32[]{:S(2)}) %all-to-all-start.1) | async-done | bytes 720928 | tf_op jit(solution)/shard_map/all_to_all | solution.py:630
  58.0 0.0 copy-start
  58.0 0.9 %copy-done = f32[128,1,1408]{2,1,0:T(1,128)} copy-done((f32[128,1,1408]{2,1,0:T(1,128)}, f32[128,1,1408]{2,1,0:T(1,128)S(1)}, u32[]{:S(2)}) %copy-start) | copy-done | bytes 720920
  58.8 4.5 %last.1 = (f32[20,4,2048]{2,1,0:T(4,128)}, f32[20,4,2048]{2,1,0:T(4,128)}, f32[2,16]{1,0:T(2,128)}) custom-call(f32[1536,128]{1,0:T(8,128)} %get-tuple-element.37.refs_0_, f32[3,4,2048]{2,1,0:T(4,128)} %refs_1_.5, s32[64,128]{1,0:T(8,128)} %get-tuple-element.27.refs_2_.refs_5_, s32[64,128]{1,0:T(8,128)} %get-tuple-element.28.refs_3_, ...), custom_call_target="tpu_custom_call" | custom-call | flops 2000000 | bytes 4000000 | tf_op jit(solution)/shard_map/last/pallas_call | solution.py:595
Async XLA Ops:
  4.0 26.5 %all-to-all-start = ((f32[128,1,1280]{2,1,0:T(1,128)}), f32[128,1,1280]{2,1,0:T(1,128)S(1)}, u32[]{:S(2)}, u32[]{:S(2)}) async-start(f32[128,1,1280]{2,1,0:T(1,128)} %get-tuple-element.34), calls=%async_computation | async-start | bytes 1310720 | tf_op jit(solution)/shard_map/all_to_all | solution.py:613
  30.6 0.8 %copy-start.1 = (f32[128,1,1280]{2,1,0:T(1,128)}, f32[128,1,1280]{2,1,0:T(1,128)S(1)}, u32[]{:S(2)}) copy-start(f32[128,1,1280]{2,1,0:T(1,128)S(1)} %all-to-all-done.refs_10_) | copy-start | bytes 1966084
  36.2 21.8 %all-to-all-start.1 = ((f32[128,1,1408]{2,1,0:T(1,128)}), f32[128,1,1408]{2,1,0:T(1,128)S(1)}, u32[]{:S(2)}, u32[]{:S(2)}) async-start(f32[128,1,1408]{2,1,0:T(1,128)} %get-tuple-element.42), calls=%async_computation.1 | async-start | bytes 1441792 | tf_op jit(solution)/shard_map/all_to_all | solution.py:630
  58.0 0.9 %copy-start = (f32[128,1,1408]{2,1,0:T(1,128)}, f32[128,1,1408]{2,1,0:T(1,128)S(1)}, u32[]{:S(2)}) copy-start(f32[128,1,1408]{2,1,0:T(1,128)S(1)} %all-to-all-done.1.refs_7_) | copy-start | bytes 2162692
